TPU v7x, 256 devices: a whole 4x4x8 slice. The times are simulated.
256 devices in a mesh: pipe: 8 (over x_lo, y), expert: 32 (over z, x_hi, core).
Axes of the slice: x: 4 (x_hi: 2, x_lo: 2; x = x_hi * 2 + x_lo), y: 4, z: 8, core: 2. Of those that a mesh axis runs over, the one named last changes fastest.
Arguments:
- tokens: bfloat16 [8, 4096, 2048], P('pipe', 'expert'), may hold values from -6 to 6
- routes: int32 [8, 4096, 6], P('pipe', 'expert'), may hold values from 0 to 31, all different within a row; in each aligned block of 128 rows (0 to 127, 128 to 255, ..., all dimensions but the last counted through in order) at most 36 rows name the same one
- norm_gain: float32 [8, 2048], P('pipe'), may hold values from 0.1 to 1.9
- router_weight: bfloat16 [8, 2048, 32], P('pipe'), may hold values from -0.125 to 0.125
- w_gate: bfloat16 [8, 32, 2048, 768], P('pipe', 'expert'), may hold values from -0.125 to 0.125
- w_up: bfloat16 [8, 32, 2048, 768], P('pipe', 'expert'), may hold values from -0.125 to 0.125
- w_down: bfloat16 [8, 32, 768, 2048], P('pipe', 'expert'), may hold values from -0.21875 to 0.21875
Outputs:
- received: bfloat16 [8, 4096, 2048], P('pipe', 'expert')
Inputs may be any that keep to these rules, and one draw needn't show every extreme that they name: Within each aligned block of 128 tokens of a section (the tokens of one device), the 6 routes of a token name different experts and no expert is named by more than 36 routes; some expert is named by exactly 36 routes in some block; every expert is named somewhere.
All inputs are finite; a program needn't handle non-finite values.
Results may differ from a plain program's by a relative error of at most 0.0039.
Values may be sent and summed in bfloat16 or wider, within the bound.
A program may use at most 128 MiB of HBM per device.

v0:
```python
import jax
import jax.numpy as jnp
from jax import lax
from jax.sharding import PartitionSpec as P


def shifted(shard, axis, by):
    devices = lax.axis_size(axis)
    return lax.ppermute(shard, axis, [(i, (i + by) % devices) for i in range(devices)])


def earlier_matrix(count):
    positions = jnp.arange(count, dtype=jnp.int32)
    return (positions[None, :] < positions[:, None]).astype(jnp.bfloat16)


def slot_ranks(route_block, experts):
    flat_routes = route_block.reshape(-1)
    hits = (flat_routes[:, None] == jnp.arange(experts, dtype=jnp.int32)[None, :]).astype(
        jnp.bfloat16
    )
    before = jnp.dot(earlier_matrix(flat_routes.shape[0]), hits, preferred_element_type=jnp.float32)
    ranks = jnp.sum(before * hits.astype(jnp.float32), axis=1).astype(jnp.int32)
    return ranks.reshape(route_block.shape)


def expert_ffn(slot_block, gate_matrix, up_matrix, down_matrix):
    gate_part = jnp.dot(slot_block, gate_matrix, preferred_element_type=jnp.float32)
    up_part = jnp.dot(slot_block, up_matrix, preferred_element_type=jnp.float32)
    hidden = (jax.nn.silu(gate_part) * up_part).astype(jnp.bfloat16)
    return jnp.dot(hidden, down_matrix, preferred_element_type=jnp.float32).astype(jnp.bfloat16)


def local(tokens, routes, norm_gain, router_weight, w_gate, w_up, w_down):
    local_rows = tokens[0]
    route_local = routes[0]
    gate_matrix = w_gate[0, 0]
    up_matrix = w_up[0, 0]
    down_matrix = w_down[0, 0]
    experts = lax.axis_size("expert")
    tok_dev, top_count = route_local.shape
    model_width = local_rows.shape[1]
    capacity = 3 * tok_dev * top_count // (2 * experts)
    wide_rows = local_rows.astype(jnp.float32)
    mean_square = jnp.mean(wide_rows * wide_rows, axis=-1, keepdims=True)
    normed = (wide_rows * lax.rsqrt(mean_square + 1e-06) * norm_gain[0]).astype(jnp.bfloat16)
    score = jax.nn.sigmoid(jnp.dot(normed, router_weight[0], preferred_element_type=jnp.float32))
    expert_ids = jnp.arange(experts, dtype=jnp.int32)
    chosen = route_local[..., None] == expert_ids[None, None, :]
    picked = jnp.sum(jnp.where(chosen, score[:, None, :], 0.0), axis=-1)
    gate_values = (picked / jnp.sum(picked, axis=1, keepdims=True)).astype(jnp.bfloat16)
    ranks = slot_ranks(route_local, experts)
    slots = route_local * capacity + ranks
    slot_hits = slots[..., None] == jnp.arange(experts * capacity, dtype=jnp.int32)[None, None, :]
    weights_map = jnp.sum(
        jnp.where(slot_hits, gate_values.astype(jnp.float32)[..., None], 0.0), axis=1
    ).astype(jnp.bfloat16)
    table = lax.all_gather(route_local, "expert", axis=0, tiled=True)
    gathered = lax.all_gather(normed, "expert", axis=0, tiled=True)
    own_index = lax.axis_index("expert")
    flat_count = tok_dev * top_count
    blocks = table.reshape(experts, flat_count)
    mine = blocks == own_index
    mine_values = mine.astype(jnp.bfloat16)
    own_ranks = jnp.dot(
        mine_values, earlier_matrix(flat_count).T, preferred_element_type=jnp.float32
    ).astype(jnp.int32)
    matches = mine[..., None] & (
        own_ranks[..., None] == jnp.arange(capacity, dtype=jnp.int32)[None, None, :]
    )
    selector = jnp.any(matches.reshape(experts, tok_dev, top_count, capacity), axis=2).astype(
        jnp.bfloat16
    )
    buffer = jnp.einsum(
        "btc,btd->bcd",
        selector,
        gathered.reshape(experts, tok_dev, model_width),
        preferred_element_type=jnp.float32,
    ).astype(jnp.bfloat16)
    owner_out = expert_ffn(buffer.reshape(-1, model_width), gate_matrix, up_matrix, down_matrix)
    returned = lax.all_to_all(
        owner_out.reshape(experts, capacity, model_width),
        "expert",
        split_axis=0,
        concat_axis=0,
        tiled=True,
    )
    moe = jnp.dot(
        weights_map,
        returned.reshape(experts * capacity, model_width),
        preferred_element_type=jnp.float32,
    )
    layer_out = (wide_rows + moe).astype(jnp.bfloat16)[None]
    received = shifted(layer_out, "pipe", 1)
    return received


def solution(mesh):
    return jax.shard_map(
        local,
        mesh=mesh,
        in_specs=(
            P("pipe", "expert", None),
            P("pipe", "expert", None),
            P("pipe", None),
            P("pipe", None, None),
            P("pipe", "expert", None, None),
            P("pipe", "expert", None, None),
            P("pipe", "expert", None, None),
        ),
        out_specs=P("pipe", "expert", None),
        check_vma=False,
    )
```

profile of v0, /device:TPU:2, one launch (start us, length us, event | category | flops | bytes accessed | tf_op | source)
XLA Modules:
  0.0 350.7 jit_solution(5233156969499989968)
XLA Ops:
  6.5 0.0 copy-start
  6.5 0.0 all-gather.3.cloned.1.call-start
  6.5 1.4 fusion.19
  7.9 2.0 fusion.21
  10.0 0.0 all-gather.3.cloned.1.call-update
  10.0 44.4 %all-gather = s32[1,4096,6]{1,0,2:T(1,128)S(1)} all-gather(s32[1,128,6]{1,0,2:T(1,128)} %param.8), channel_id=2, replica_groups=mesh['pipe'=8,'expert'=32] {'expert'}, dimensions={1}, use_global_device_ids=true | all-gather | bytes 101376 | tf_op jit(solution)/shard_map/all_gather | solution.py:58
  54.4 0.9 fusion.35
  55.3 1.5 copy.23
  56.8 2.5 eq.86
  59.3 1.0 fusion.14
  60.3 1.1 copy.24
  61.4 0.8 eq.87
  62.2 1.2 copy.25
  63.4 0.8 copy.33
  64.2 0.5 fusion.1
  64.7 85.4 %all-gather.3.cloned.1.call-done = bf16[4096,2048]{1,0:T(8,128)(2,1)} async-done(((bf16[128,2048]{1,0:T(8,128)(2,1)}), bf16[4096,2048]{1,0:T(8,128)(2,1)}) %all-gather.3.cloned.1.call-update) | async-done | bytes 16777232 | tf_op jit(solution)/shard_map/all_gather | solution.py:59
  150.0 10.4 %convolution_convert_fusion.1 = bf16[32,36,2048]{2,1,0:T(8,128)(2,1)} fusion(bf16[32,128,2048]{2,1,0:T(8,128)(2,1)} %bitcast.55, pred[32,128,36]{1,0,2:T(8,128)(4,1)S(1)} %fusion.1), kind=kOutput, calls=%fused_computation.1 | convolution fusion | flops 606339072 | bytes 21643264 | tf_op jit(solution)/shard_map/btc,btd->bcd/dot_general | solution.py:74
  160.4 7.2 %reshape.90 = bf16[1152,2048]{1,0:T(8,128)(2,1)} reshape(bf16[32,36,2048]{2,1,0:T(8,128)(2,1)} %convolution_convert_fusion.1) | data formatting | bytes 9437184 | tf_op jit(solution)/shard_map/reshape | solution.py:80
  167.7 0.0 copy-start.1
  167.7 0.0 copy-start.4
  167.7 6.8 %fusion.5 = f32[1152,768]{1,0:T(8,128)S(1)} fusion(bf16[1152,2048]{1,0:T(8,128)(2,1)} %reshape.90, bf16[1,1,2048,768]{3,2,1,0:T(8,128)(2,1)} %param.11), kind=kOutput, calls=%fused_computation.11 | convolution fusion | flops 3623878656 | bytes 11403264 | tf_op jit(solution)/shard_map/dot_general | solution.py:28
  174.4 0.0 copy-done.1
  174.4 0.0 copy-done.4
  174.4 4.2 %fusion.2 = bf16[1152,768]{1,0:T(8,128)(2,1)S(1)} fusion(bf16[1152,2048]{1,0:T(8,128)(2,1)S(1)} %copy-done.1, f32[1152,768]{1,0:T(8,128)S(1)} %fusion.5, bf16[1,1,2048,768]{3,2,1,0:T(8,128)(2,1)S(1)} %copy-done.4), kind=kOutput, calls=%fused_computation.8 | convolution fusion | flops 3629187072 | bytes 13172736 | tf_op jit(solution)/shard_map/dot_general | solution.py:29
  178.6 0.0 copy-done
  178.6 5.5 %convolution_convert_fusion = bf16[1152,2048]{1,0:T(8,128)(2,1)} fusion(bf16[1152,768]{1,0:T(8,128)(2,1)S(1)} %fusion.2, bf16[1,1,768,2048]{3,2,1,0:T(8,128)(2,1)S(1)} %copy-done), kind=kOutput, calls=%fused_computation | convolution fusion | flops 3626237952 | bytes 9633792 | tf_op jit(solution)/shard_map/dot_general | solution.py:31
  184.2 7.2 %reshape.91 = bf16[32,36,2048]{2,1,0:T(8,128)(2,1)} reshape(bf16[1152,2048]{1,0:T(8,128)(2,1)} %convolution_convert_fusion) | data formatting | bytes 9437184 | tf_op jit(solution)/shard_map/reshape | solution.py:82
  191.4 0.0 copy-start.2
  191.4 0.0 copy-start.3
  191.4 5.8 %all-to-all-start = ((bf16[32,36,2048]{2,1,0:T(8,128)(2,1)}), bf16[32,36,2048]{2,1,0:T(8,128)(2,1)}, u32[]{:S(2)}, u32[]{:S(2)}) async-start(bf16[32,36,2048]{2,1,0:T(8,128)(2,1)} %reshape.91), calls=%async_computation | async-start | bytes 10485760 | tf_op jit(solution)/shard_map/all_to_all | solution.py:81
  197.2 0.0 copy-done.2
  197.2 0.1 copy.19
  197.3 0.1 eq.73
  197.5 0.4 fusion.15
  197.8 0.1 convert_element_type.75
  198.0 0.1 copy.21
  198.1 0.0 copy-done.3
  198.1 1.5 fusion.18
  199.6 0.5 select_reduce_fusion
  200.1 116.3 %all-to-all-done = bf16[32,36,2048]{2,1,0:T(8,128)(2,1)} async-done(((bf16[32,36,2048]{2,1,0:T(8,128)(2,1)}), bf16[32,36,2048]{2,1,0:T(8,128)(2,1)}, u32[]{:S(2)}, u32[]{:S(2)}) %all-to-all-start) | async-done | bytes 4718624 | tf_op jit(solution)/shard_map/all_to_all | solution.py:81
  316.4 7.2 %reshape.92 = bf16[1152,2048]{1,0:T(8,128)(2,1)} reshape(bf16[32,36,2048]{2,1,0:T(8,128)(2,1)} %all-to-all-done) | data formatting | bytes 9437184 | tf_op jit(solution)/shard_map/reshape | solution.py:90
  323.6 3.3 fusion.10
  326.9 1.6 collective-permute-start
  328.5 14.5 %collective-permute-done = bf16[1,128,2048]{2,1,0:T(8,128)(2,1)S(1)} collective-permute-done((bf16[1,128,2048]{2,1,0:T(8,128)(2,1)S(1)}, bf16[1,128,2048]{2,1,0:T(8,128)(2,1)S(1)}, u32[]{:S(2)}, u32[]{:S(2)}) %collective-permute-start) | collective-permute-done | bytes 524320 | tf_op jit(solution)/shard_map/ppermute | solution.py:9
  343.0 0.8 copy.37
  (6 shorter events, 0.1 us)
Async XLA Ops:
  6.5 172.1 %copy-start = (bf16[1,1,768,2048]{3,2,1,0:T(8,128)(2,1)S(1)}, bf16[1,1,768,2048]{3,2,1,0:T(8,128)(2,1)}, u32[]{:S(2)}) copy-start(bf16[1,1,768,2048]{3,2,1,0:T(8,128)(2,1)} %param.13) | copy-start | bytes 9437188
  6.5 143.5 %all-gather.3.cloned.1.call-start = ((), (), s32[]{:S(2)}) async-start(), calls=%async_computation.1 | async-start | bytes 17301504 | tf_op jit(solution)/shard_map/all_gather | solution.py:59
  167.7 6.8 %copy-start.1 = (bf16[1152,2048]{1,0:T(8,128)(2,1)S(1)}, bf16[1152,2048]{1,0:T(8,128)(2,1)}, u32[]{:S(2)}) copy-start(bf16[1152,2048]{1,0:T(8,128)(2,1)} %reshape.90) | copy-start | bytes 14155780
  167.7 6.8 %copy-start.4 = (bf16[1,1,2048,768]{3,2,1,0:T(8,128)(2,1)S(1)}, bf16[1,1,2048,768]{3,2,1,0:T(8,128)(2,1)}, u32[]{:S(2)}) copy-start(bf16[1,1,2048,768]{3,2,1,0:T(8,128)(2,1)} %param.12) | copy-start | bytes 9437188
  191.4 5.8 %copy-start.2 = (s32[1,128,6]{1,0,2:T(1,128)S(1)}, s32[1,128,6]{1,0,2:T(1,128)}, u32[]{:S(2)}) copy-start(s32[1,128,6]{1,0,2:T(1,128)} %param.8) | copy-start | bytes 9220
  191.4 6.7 %copy-start.3 = (f32[1,2048]{1,0:T(1,128)S(1)}, f32[1,2048]{1,0:T(1,128)}, u32[]{:S(2)}) copy-start(f32[1,2048]{1,0:T(1,128)} %param.9) | copy-start | bytes 24580
  191.4 125.0 %all-to-all-start = ((bf16[32,36,2048]{2,1,0:T(8,128)(2,1)}), bf16[32,36,2048]{2,1,0:T(8,128)(2,1)}, u32[]{:S(2)}, u32[]{:S(2)}) async-start(bf16[32,36,2048]{2,1,0:T(8,128)(2,1)} %reshape.91), calls=%async_computation | async-start | bytes 10485760 | tf_op jit(solution)/shard_map/all_to_all | solution.py:81
  326.9 16.1 %collective-permute-start = (bf16[1,128,2048]{2,1,0:T(8,128)(2,1)S(1)}, bf16[1,128,2048]{2,1,0:T(8,128)(2,1)S(1)}, u32[]{:S(2)}, u32[]{:S(2)}) collective-permute-start(bf16[1,128,2048]{2,1,0:T(8,128)(2,1)S(1)} %fusion.10), channel_id=1, source_target_pairs={{0,32},{32,64},{64,96},{96,128},{128,160},{160,192},{192,224},{224... | collective-permute-start | bytes 1572872 | tf_op jit(solution)/shard_map/ppermute | solution.py:9
Sparse Core Ops, SparseCore 0:
  10.1 139.8 all-gather.2
where the time goes:
time: 352 us; the launch traced here: 351 us
  waiting for transfers between devices  216 us (61%)
  blocking collectives  44.4 us (13%)
  matrix products  32.9 us (9%)
  local copies, waits for them, and re-layouts  30.8 us (9%)
  between operations  13.5 us (4%)
  starting transfers between devices  7.39 us (2%)
  other arithmetic  5.4 us (2%)
    all_to_all x1, waiting for transfers between devices, local(): lax.all_to_all(owner_out.reshape(experts, capacity, model_width), 'expert...  116 us
    all_gather x1, waiting for transfers between devices, local(): gathered = lax.all_gather(normed, 'expert', axis=0, tiled=True)  85.4 us
    all_gather x1, blocking collectives, local(): table = lax.all_gather(route_local, 'expert', axis=0, tiled=True)  44.4 us
    ppermute x1, waiting for transfers between devices, shifted(): lax.ppermute(shard, axis, [(i, (i + by) % devices) for i in range(devices)])  14.5 us
    dot_general x1, matrix products, local(): jnp.einsum('btc,btd->bcd', selector, gathered.reshape(experts, tok_dev, m...  10.4 us
    reshape x1, local copies, waits for them, and re-layouts, local(): buffer.reshape(-1, model_width)  7.24 us
    reshape x1, local copies, waits for them, and re-layouts, local(): returned.reshape(experts * capacity, model_width)  7.22 us
    reshape x1, local copies, waits for them, and re-layouts, local(): owner_out.reshape(experts, capacity, model_width)  7.21 us
  transfers between devices with their start and end apart: 3, of which 3 were waited for; matrix products, arithmetic and copies ran while one was open for 4% of the time, Pallas kernels for 0%

commit v1 on v0

v1 whole, which is shorter than its diff:
```python
import functools

import jax
import jax.numpy as jnp
from jax import lax
from jax.experimental import pallas as pl
from jax.experimental.pallas import tpu as pltpu
from jax.sharding import PartitionSpec as P

MESH = pl.DeviceIdType.MESH
NZ = 8
CAP = 36
GROUP = 4
ROWS = GROUP * CAP
FAR = 1024.0
SLOT = {0: 0, -1: 1, 1: 2, -2: 3, 2: 4, -3: 5, 3: 6, 4: 7, -4: 7}


def kernel(
    nq, tokens, routes, gain, router, wg_hbm, wu_hbm, wd_hbm, out,
    xb, pts, pt, sel, wmap, so, xs, yr, acc_g, acc_u, hid, cb, rss, rsr, outs, wg, wu, wd,
    zs_s, zs_r, pt_s, pt_r, xs_s, xs_r, ys_s, ys_r, rs_s, rs_r, pp_s, pp_r, w_sem,
):
    width = tokens.shape[2]
    tok = tokens.shape[1]
    half = tok // 2
    F = width // nq
    p = lax.axis_index("pipe")
    e = lax.axis_index("expert")
    z, a, c = e // 4, (e // 2) % 2, e % 2
    mine = 2 * a + c

    def at_z(d):
        return {"expert": ((z + d + NZ) % NZ) * 4 + mine}

    level = [mine, 2 * a + (1 - c), 2 * (1 - a) + c, 2 * (1 - a) + (1 - c)]

    def at_level(t):
        return {"expert": z * 4 + level[t]}

    barrier = pltpu.get_barrier_semaphore()
    for d in range(1, NZ):
        pl.semaphore_signal(barrier, inc=1, device_id=at_z(d), device_id_type=MESH)
    for t in (1, 2, 3):
        pl.semaphore_signal(barrier, inc=1, device_id=at_level(t), device_id_type=MESH)
    pl.semaphore_signal(barrier, inc=1, device_id={"pipe": (p + 7) % 8}, device_id_type=MESH)

    w_copies = [
        pltpu.make_async_copy(wg_hbm.at[0, 0], wg, w_sem.at[0]),
        pltpu.make_async_copy(wu_hbm.at[0, 0], wu, w_sem.at[1]),
        pltpu.make_async_copy(wd_hbm.at[0, 0], wd, w_sem.at[2]),
    ]
    for w_copy in w_copies:
        w_copy.start()

    def remote(src, dst, s_sem, r_sem, where):
        return pltpu.make_async_remote_copy(
            src_ref=src, dst_ref=dst, send_sem=s_sem, recv_sem=r_sem, device_id=where, device_id_type=MESH
        )

    def z_copy(q, way, s):
        sign = 1 - 2 * way
        src, dst = xb.at[q, SLOT[-(s - 1) * sign]], xb.at[q, SLOT[-s * sign]]
        if s == 4:
            part = pl.ds(way * half, half)
            src, dst = src.at[part], dst.at[part]
        return remote(src, dst, zs_s.at[q, way, s - 1], zs_r.at[q, way, s - 1], at_z(sign))

    def pt_copy(d):
        return remote(pts.at[(z + d + NZ) % NZ], pt.at[SLOT[-d]], pt_s.at[SLOT[-d]], pt_r.at[SLOT[-d]], at_z(d))

    def x_copy(q, t):
        return remote(so.at[q, level[t]], xs.at[q, mine], xs_s.at[q, t], xs_r.at[q, t], at_level(t))

    def x_own(q):
        return pltpu.make_async_copy(so.at[q, mine], xs.at[q, mine], xs_r.at[q, 0])

    def y_copy(q, t):
        return remote(so.at[q, level[t]], yr.at[q, :, mine], ys_s.at[q, t], ys_r.at[q, t], at_level(t))

    def y_own(q):
        return pltpu.make_async_copy(so.at[q, mine], yr.at[q, :, mine], ys_r.at[q, 0])

    def rs_copy(q, way, s):
        sign = 1 - 2 * way
        src, dst = rss.at[q, way, s], rsr.at[q, way, s]
        if s == 0:
            part = pl.ds(way * half, half)
            src, dst = src.at[part], dst.at[part]
        return remote(src, dst, rs_s.at[q, way, s], rs_r.at[q, way, s], at_z(sign))

    def pipe_copy(q):
        return remote(
            outs.at[q], out.at[0, :, pl.ds(pl.multiple_of(q * F, F), F)], pp_s.at[q], pp_r.at[q], {"pipe": (p + 1) % 8}
        )

    wide = tokens[0].astype(jnp.float32)
    mean_square = jnp.mean(wide * wide, axis=-1, keepdims=True)
    normed = (wide * lax.rsqrt(mean_square + 1e-06) * gain[...]).astype(jnp.bfloat16)
    for q in range(nq):
        xb[q, 0] = normed[:, q * F : (q + 1) * F]

    pl.semaphore_wait(barrier, 11)
    for way in (0, 1):
        z_copy(0, way, 1).start()

    lane = lax.broadcasted_iota(jnp.int32, (1, 16 * NZ), 1)
    kind = lane % 16
    expert_of = 4 * (lane // 16) + lane % 4
    spread = (lax.broadcasted_iota(jnp.int32, (router.shape[2], 16 * NZ), 0) == expert_of).astype(jnp.bfloat16)
    wide_router = jnp.dot(router[0], spread, preferred_element_type=jnp.float32).astype(jnp.bfloat16)
    score = jax.nn.sigmoid(jnp.dot(normed, wide_router, preferred_element_type=jnp.float32))
    hit = jnp.zeros((tok, 16 * NZ), jnp.float32)
    for k in range(routes.shape[2]):
        hit = hit + (routes[0, :, k : k + 1] == expert_of).astype(jnp.float32)
    earlier = (
        lax.broadcasted_iota(jnp.int32, (tok, tok), 1) < lax.broadcasted_iota(jnp.int32, (tok, tok), 0)
    ).astype(jnp.bfloat16)
    rank = jnp.dot(earlier, hit.astype(jnp.bfloat16), preferred_element_type=jnp.float32)
    total = jnp.sum(jnp.where(kind < 4, hit * score, 0.0), axis=1, keepdims=True)
    gate = score / total
    packed = jnp.where(
        kind < 4, jnp.where(hit > 0.0, rank, FAR), jnp.where((kind < 8) & (hit > 0.0), gate, 0.0)
    )
    pts[...] = jnp.transpose(packed).astype(jnp.bfloat16).reshape(NZ, 16, tok)
    for d in range(1, NZ):
        pt_copy(d if d <= 4 else d - NZ).start()
    pt[0] = pts[z]

    def build_sel():
        for d in range(1, NZ):
            pt_copy(d if d <= 4 else d - NZ).wait_recv()
        row = lax.broadcasted_iota(jnp.int32, (ROWS, tok), 0).astype(jnp.float32)
        for g in range(2):
            for i in range(GROUP):
                tile = pt[g * GROUP + i].astype(jnp.float32)
                for j in range(4):
                    same = (row - float(CAP * i)) == tile[j : j + 1, :]
                    sel[g, j * ROWS : (j + 1) * ROWS, i * tok : (i + 1) * tok] = jnp.where(same, 1.0, 0.0).astype(
                        jnp.bfloat16
                    )

    def build_wmap():
        turned = jnp.transpose(pt[...].reshape(16 * NZ, tok).astype(jnp.float32))
        col = lax.broadcasted_iota(jnp.int32, (tok, 4 * ROWS), 1).astype(jnp.float32)
        for g in range(2):
            for i in range(GROUP):
                first = (g * GROUP + i) * 16
                value = jnp.zeros((tok, 4 * ROWS), jnp.float32)
                for j in range(4):
                    place = turned[:, first + j : first + j + 1] + float(ROWS * j + CAP * i)
                    weight = turned[:, first + 4 + j : first + 5 + j]
                    value = jnp.where(col == place, weight, value)
                wmap[g, i * tok : (i + 1) * tok] = value.astype(jnp.bfloat16)

    def valid(q, body):
        @pl.when((q >= 0) & (q < nq))
        def _():
            body(q)

    def forward(s):
        def body(q):
            for way in (0, 1):
                if s > 1:
                    z_copy(q, way, s - 1).wait_recv()
                z_copy(q, way, s).start()

        return body

    def select(q):
        for way in (0, 1):
            z_copy(q, way, 4).wait_recv()
        for g in range(2):
            block = xb[q, g * GROUP : (g + 1) * GROUP].reshape(GROUP * tok, F)
            picked = jnp.dot(sel[g], block, preferred_element_type=jnp.float32).astype(jnp.bfloat16)
            for j in range(4):
                so[q, j, g] = picked[j * ROWS : (j + 1) * ROWS]
        for t in (2, 3, 1):
            x_copy(q, t).start()
        x_own(q).start()

    def accumulate(q):
        for t in (1, 2, 3):
            x_copy(q, t).wait_recv()
        x_own(q).wait()
        rows = xs[q].reshape(8 * ROWS, F)
        part = pl.ds(pl.multiple_of(q * F, F), F)
        acc_g[...] += jnp.dot(rows, wg[part], preferred_element_type=jnp.float32)
        acc_u[...] += jnp.dot(rows, wu[part], preferred_element_type=jnp.float32)

    LAG = 1

    def gather_tick(tau, carry):
        valid(tau - 4, select)
        for s in (4, 3, 2):
            valid(tau - s + 1, forward(s))

        @pl.when(tau > 0)
        def _():
            valid(tau, forward(1))

        valid(tau - 4 - LAG, accumulate)
        return carry

    lax.fori_loop(0, 4, gather_tick, 0)
    build_sel()
    acc_g[...] = jnp.zeros_like(acc_g)
    acc_u[...] = jnp.zeros_like(acc_u)
    for w_copy in w_copies:
        w_copy.wait()
    lax.fori_loop(4, 6, gather_tick, 0)
    build_wmap()
    lax.fori_loop(6, nq + 4 + LAG, gather_tick, 0)

    def act(k, carry):
        part = pl.ds(pl.multiple_of(k * ROWS, ROWS), ROWS)
        v = acc_g[part]
        hid[part] = (v / (1.0 + jnp.exp(-v)) * acc_u[part]).astype(jnp.bfloat16)
        return carry

    lax.fori_loop(0, 8, act, 0)

    def sent(q, carry):
        for t in (1, 2, 3):
            x_copy(q, t).wait_send()
        return carry

    lax.fori_loop(0, nq, sent, 0)

    def produce(q):
        part = pl.ds(pl.multiple_of(q * F, F), F)
        y = jnp.dot(hid[...], wd[:, part], preferred_element_type=jnp.float32).astype(jnp.bfloat16)
        for k in range(4):
            for g in range(2):
                n = (2 * k + g) * ROWS
                so[q, k, g] = y[n : n + ROWS]
        for t in (2, 3, 1):
            y_copy(q, t).start()
        y_own(q).start()

    def unselect(q):
        for t in (1, 2, 3):
            y_copy(q, t).wait_recv()
        y_own(q).wait()
        for g in (1, 0):
            rows = yr[q, g].reshape(4 * ROWS, F)
            sums = jnp.dot(wmap[g], rows, preferred_element_type=jnp.float32)
            for i in range(GROUP):
                block = sums[i * tok : (i + 1) * tok]
                if g * GROUP + i == 7:
                    rss[q, 0, 0] = block.astype(jnp.bfloat16)
                    rss[q, 1, 0] = block.astype(jnp.bfloat16)
                else:
                    cb[q, g * GROUP + i] = block
            if g == 1:
                for way in (0, 1):
                    rs_copy(q, way, 0).start()

    def pass_on(s):
        def body(q):
            for way in (0, 1):
                rs_copy(q, way, s - 1).wait_recv()
                sign = 1 - 2 * way
                slot = SLOT[(4 - s) * sign]
                if s == 1:
                    add, keep = slice(way * half, (way + 1) * half), slice((1 - way) * half, (2 - way) * half)
                    rss[q, way, s, add] = (
                        cb[q, slot, add] + rsr[q, way, s - 1, add].astype(jnp.float32)
                    ).astype(jnp.bfloat16)
                    rss[q, way, s, keep] = cb[q, slot, keep].astype(jnp.bfloat16)
                else:
                    rss[q, way, s] = (cb[q, slot] + rsr[q, way, s - 1].astype(jnp.float32)).astype(jnp.bfloat16)
                rs_copy(q, way, s).start()

        return body

    def finish(q):
        for way in (0, 1):
            rs_copy(q, way, 3).wait_recv()
        part = pl.ds(pl.multiple_of(q * F, F), F)
        moe = cb[q, 0] + rsr[q, 0, 3].astype(jnp.float32) + rsr[q, 1, 3].astype(jnp.float32)
        outs[q] = (tokens[0, :, part].astype(jnp.float32) + moe).astype(jnp.bfloat16)
        pipe_copy(q).start()

    LEAD = 2
    for q in range(LEAD):
        produce(q)

    def combine_tick(tau, carry):
        valid(tau - 4, finish)
        for s in (3, 2, 1):
            valid(tau - s, pass_on(s))
        valid(tau, unselect)

        @pl.when(tau + LEAD < nq)
        def _():
            produce(tau + LEAD)

        return carry

    lax.fori_loop(0, nq + 4, combine_tick, 0)

    def drain(q, carry):
        for way in (0, 1):
            for s in range(1, 5):
                z_copy(q, way, s).wait_send()
            for s in range(4):
                rs_copy(q, way, s).wait_send()
        for t in (1, 2, 3):
            y_copy(q, t).wait_send()
        pipe_copy(q).wait()
        return carry

    for d in range(1, NZ):
        pt_copy(d if d <= 4 else d - NZ).wait_send()
    lax.fori_loop(0, nq, drain, 0)


def local(tokens, routes, norm_gain, router_weight, w_gate, w_up, w_down):
    tok, width = tokens.shape[1:]
    ff = w_gate.shape[3]
    nq = 8
    F = width // nq
    bf, f32 = jnp.bfloat16, jnp.float32
    vmem = pl.BlockSpec(memory_space=pltpu.VMEM)
    anywhere = pl.BlockSpec(memory_space=pl.ANY)
    dma = pltpu.SemaphoreType.DMA
    return pl.pallas_call(
        functools.partial(kernel, nq),
        out_shape=jax.ShapeDtypeStruct(tokens.shape, bf),
        in_specs=[vmem, vmem, vmem, vmem, anywhere, anywhere, anywhere],
        out_specs=anywhere,
        scratch_shapes=[
            pltpu.VMEM((nq, NZ, tok, F), bf),
            pltpu.VMEM((NZ, 16, tok), bf),
            pltpu.VMEM((NZ, 16, tok), bf),
            pltpu.VMEM((2, 4 * ROWS, GROUP * tok), bf),
            pltpu.VMEM((2, GROUP * tok, 4 * ROWS), bf),
            pltpu.VMEM((nq, 4, 2, ROWS, F), bf),
            pltpu.VMEM((nq, 4, 2, ROWS, F), bf),
            pltpu.VMEM((nq, 2, 4, ROWS, F), bf),
            pltpu.VMEM((8 * ROWS, ff), f32),
            pltpu.VMEM((8 * ROWS, ff), f32),
            pltpu.VMEM((8 * ROWS, ff), bf),
            pltpu.VMEM((nq, 7, tok, F), f32),
            pltpu.VMEM((nq, 2, 4, tok, F), bf),
            pltpu.VMEM((nq, 2, 4, tok, F), bf),
            pltpu.VMEM((nq, tok, F), bf),
            pltpu.VMEM((width, ff), bf),
            pltpu.VMEM((width, ff), bf),
            pltpu.VMEM((ff, width), bf),
            dma((nq, 2, 4)),
            dma((nq, 2, 4)),
            dma((NZ,)),
            dma((NZ,)),
            dma((nq, 4)),
            dma((nq, 4)),
            dma((nq, 4)),
            dma((nq, 4)),
            dma((nq, 2, 4)),
            dma((nq, 2, 4)),
            dma((nq,)),
            dma((nq,)),
            dma((3,)),
        ],
        compiler_params=pltpu.CompilerParams(
            collective_id=0, has_side_effects=True, vmem_limit_bytes=62 * 2**20
        ),
        name="relay_moe",
    )(tokens, routes, norm_gain, router_weight, w_gate, w_up, w_down)


def solution(mesh):
    return jax.shard_map(
        local,
        mesh=mesh,
        in_specs=(
            P("pipe", "expert", None),
            P("pipe", "expert", None),
            P("pipe", None),
            P("pipe", None, None),
            P("pipe", "expert", None, None),
            P("pipe", "expert", None, None),
            P("pipe", "expert", None, None),
        ),
        out_specs=P("pipe", "expert", None),
        check_vma=False,
    )
```

time: 352 us -> 167 us (0.47)
  waiting for transfers between devices: 216 us -> 0 us
  Pallas kernels: 0 us -> 161 us
  blocking collectives: 44.4 us -> 0 us
  matrix products: 32.9 us -> 0 us
  local copies, waits for them, and re-layouts: 30.8 us -> 5.2 us
  between operations: 13.5 us -> 0.01 us
  starting transfers between devices: 7.39 us -> 0 us
  other arithmetic: 5.4 us -> 0 us
    pallas_call x0 -> x1, Pallas kernels: none -> 161 us  [local(): pl.pallas_call(functools.partial(kernel, nq), out_shape=jax.ShapeDtypeStr...]
    all_to_all x1 -> x0, waiting for transfers between devices: 116 us -> none  [local(): lax.all_to_all(owner_out.reshape(experts, capacity, model_width), 'expert...]
    all_gather x1 -> x0, waiting for transfers between devices: 85.4 us -> none  [local(): gathered = lax.all_gather(normed, 'expert', axis=0, tiled=True)]
    all_gather x1 -> x0, blocking collectives: 44.4 us -> none  [local(): table = lax.all_gather(route_local, 'expert', axis=0, tiled=True)]
    dot_general x8 -> x0, matrix products: 32.9 us -> none  [the longest x1 10.4 us: local(): jnp.einsum('btc,btd->bcd', selector, gathered.reshape(experts, tok_dev, m...]
    reshape x3 -> x0, local copies, waits for them, and re-layouts: 21.7 us -> none  [the longest x1 7.24 us: local(): buffer.reshape(-1, model_width)]
    ppermute x1 -> x0, waiting for transfers between devices: 14.5 us -> none  [shifted(): lax.ppermute(shard, axis, [(i, (i + by) % devices) for i in range(devices)])]
    eq x5 -> x0, local copies, waits for them, and re-layouts: 6.17 us -> none  [the longest x2 4.01 us: local(): mine = blocks == own_index]
  transfers between devices with their start and end apart: 3 -> 0, of which waited for: 3 -> 0; matrix products, arithmetic and copies ran while one was open for 4% -> 0% of each run, Pallas kernels for 0% -> 0%
where the time goes in v1:
time: 167 us; the launch traced here: 166 us
  Pallas kernels  161 us (96%)
  local copies, waits for them, and re-layouts  5.2 us (3%)
    pallas_call x1, Pallas kernels, local(): pl.pallas_call(functools.partial(kernel, nq), out_shape=jax.ShapeDtypeStr...  161 us
    unnamed x3, local copies, waits for them, and re-layouts  5.2 us

profile of v1, /device:TPU:2, one launch (start us, length us, event | category | flops | bytes accessed | tf_op | source)
XLA Modules:
  0.0 166.5 jit_solution(6777861764583414693)
XLA Ops:
  0.0 1.4 copy.8.routes
  1.4 1.9 %copy.9.router = bf16[1,2048,32]{2,1,0:T(8,128)(2,1)} copy(bf16[1,2048,32]{1,2,0:T(8,128)(2,1)} %param.10) | data formatting | bytes 262144 | tf_op args[3]
  3.3 161.3 %relay_moe.1 = bf16[1,128,2048]{2,1,0:T(8,128)(2,1)} custom-call(bf16[1,128,2048]{2,1,0:T(8,128)(2,1)} %tokens.1, s32[1,128,6]{2,1,0:T(8,128)} %copy.8.routes, f32[1,2048]{1,0:T(1,128)} %gain.1, bf16[1,2048,32]{2,1,0:T(8,128)(2,1)} %copy.9.router, bf16[1,1,2048,768]{3,2,1,0:T(8,128)(2,1)} %wg_hbm.1, bf16[1,1,2048,768]{3,2,1,0:T(8,128)(2,1)} %wu_hbm.1, ...), custom_call_target="tpu_custom_call" | custom-call | tf_op jit(solution)/shard_map/relay_moe/pallas_call | solution.py:328
  164.6 1.9 %copy.11 = bf16[1,128,2048]{2,1,0:T(8,128)(2,1)} copy(bf16[1,128,2048]{2,1,0:T(8,128)(2,1)} %relay_moe.1) | data formatting | bytes 1048576

commit v2 on v1

v2 whole, which is shorter than its diff:
```python
import functools

import jax
import jax.numpy as jnp
from jax import lax
from jax.experimental import pallas as pl
from jax.experimental.pallas import tpu as pltpu
from jax.sharding import PartitionSpec as P

MESH = pl.DeviceIdType.MESH
NZ = 8
CAP = 36
GROUP = 4
ROWS = GROUP * CAP
KEPT = 4
FAR = 1024.0
SLOT = {0: 0, -1: 1, 1: 2, -2: 3, 2: 4, -3: 5, 3: 6, 4: 7, -4: 7}


def kernel(
    nq, tokens, routes, gain, router, wg_hbm, wu_hbm, wd_hbm, out,
    xb, xe, pts, pt, sel, wmap, sel_e, wmap_e, so, xs, yr, yr_e, acc_g, acc_u, hid, cb, cb_e, rss, rsr, rss_e, rsr_e,
    last, outs, wg, wu, wd,
    zs_s, zs_r, pt_s, pt_r, xs_s, xs_r, ys_s, ys_r, rs_s, rs_r, ex_s, ex_r, pp_s, pp_r, w_sem,
):
    width = tokens.shape[2]
    tok = tokens.shape[1]
    half = tok // 2
    F = width // nq
    E = nq - 1
    p = lax.axis_index("pipe")
    e = lax.axis_index("expert")
    z, a, c = e // 4, (e // 2) % 2, e % 2
    mine = 2 * a + c

    def at_z(d):
        return {"expert": ((z + d + NZ) % NZ) * 4 + mine}

    def across(d):
        return {"expert": ((z + d + NZ) % NZ) * 4 + 2 * (1 - a) + c}

    level = [mine, 2 * a + (1 - c), 2 * (1 - a) + c, 2 * (1 - a) + (1 - c)]

    def at_level(t):
        return {"expert": z * 4 + level[t]}

    barrier = pltpu.get_barrier_semaphore()
    for d in range(1, NZ):
        pl.semaphore_signal(barrier, inc=1, device_id=at_z(d), device_id_type=MESH)
        pl.semaphore_signal(barrier, inc=1, device_id=across(d), device_id_type=MESH)
    for t in (1, 2, 3):
        pl.semaphore_signal(barrier, inc=1, device_id=at_level(t), device_id_type=MESH)
    pl.semaphore_signal(barrier, inc=1, device_id={"pipe": (p + 7) % 8}, device_id_type=MESH)

    w_copies = [
        pltpu.make_async_copy(wg_hbm.at[0, 0], wg, w_sem.at[0]),
        pltpu.make_async_copy(wu_hbm.at[0, 0], wu, w_sem.at[1]),
        pltpu.make_async_copy(wd_hbm.at[0, 0], wd, w_sem.at[2]),
    ]
    for w_copy in w_copies:
        w_copy.start()

    def remote(src, dst, s_sem, r_sem, where):
        return pltpu.make_async_remote_copy(
            src_ref=src, dst_ref=dst, send_sem=s_sem, recv_sem=r_sem, device_id=where, device_id_type=MESH
        )

    def z_copy(q, way, s):
        sign = 1 - 2 * way
        src, dst = xb.at[q, SLOT[-(s - 1) * sign]], xb.at[q, SLOT[-s * sign]]
        if s == 4:
            part = pl.ds(way * half, half)
            src, dst = src.at[part], dst.at[part]
        return remote(src, dst, zs_s.at[q, way, s - 1], zs_r.at[q, way, s - 1], at_z(sign))

    def ze_copy(way, s):
        sign = 1 - 2 * way
        src, dst = xe.at[:, SLOT[-(s - 1) * sign]], xe.at[:, SLOT[-s * sign]]
        if s == 4:
            part = pl.ds(way * half, half)
            src, dst = src.at[:, part], dst.at[:, part]
        return remote(src, dst, zs_s.at[E, way, s - 1], zs_r.at[E, way, s - 1], at_z(sign))

    def pt_copy(d, col):
        n = SLOT[-d] if d else 0
        return remote(
            pts.at[(z + d + NZ) % NZ], pt.at[col, n], pt_s.at[col, n], pt_r.at[col, n], across(d) if col else at_z(d)
        )

    pt_all = [(d, col) for d in (1, -1, 2, -2, 3, -3, 4, 0) for col in (0, 1) if d or col]

    def x_copy(q, t, g):
        return remote(
            so.at[q, level[t], g], xs.at[q, a, c, g], xs_s.at[q, t, g], xs_r.at[q, t, g], at_level(t)
        )

    def x_own(q, g):
        return pltpu.make_async_copy(so.at[q, mine, g], xs.at[q, a, c, g], xs_r.at[q, 0, g])

    def xe_copy():
        return remote(
            so.at[E, pl.ds(2 * (1 - c), 2)], xs.at[E, :, c], xs_s.at[E, 1, 0], xs_r.at[E, 1, 0], at_level(1)
        )

    def xe_own():
        return pltpu.make_async_copy(so.at[E, pl.ds(2 * c, 2)], xs.at[E, :, c], xs_r.at[E, 0, 0])

    def y_copy(q, t, g):
        return remote(so.at[q, level[t], g], yr.at[q, g, mine], ys_s.at[q, t, g], ys_r.at[q, t, g], at_level(t))

    def y_own(q, g):
        return pltpu.make_async_copy(so.at[q, mine, g], yr.at[q, g, mine], ys_r.at[q, 0, g])

    def ye_copy():
        return remote(
            so.at[E, pl.ds(2 * (1 - c), 2)], yr_e.at[:, :, c], ys_s.at[E, 1, 0], ys_r.at[E, 1, 0], at_level(1)
        )

    def ye_own():
        return pltpu.make_async_copy(so.at[E, pl.ds(2 * c, 2)], yr_e.at[:, :, c], ys_r.at[E, 0, 0])

    def early_copy():
        return remote(xe.at[0, 0], xe.at[1, 0], ex_s.at[0], ex_r.at[0], at_level(2))

    def late_copy():
        return remote(last.at[0], last.at[1], ex_s.at[1], ex_r.at[1], at_level(2))

    def rs_copy(q, way, s):
        sign = 1 - 2 * way
        src, dst = rss.at[q, way, s], rsr.at[q, way, s]
        if s == 0:
            part = pl.ds(way * half, half)
            src, dst = src.at[part], dst.at[part]
        return remote(src, dst, rs_s.at[q, way, s], rs_r.at[q, way, s], at_z(sign))

    def rse_copy(way, s):
        sign = 1 - 2 * way
        src, dst = rss_e.at[way, s], rsr_e.at[way, s]
        if s == 0:
            part = pl.ds(way * half, half)
            src, dst = src.at[:, part], dst.at[:, part]
        return remote(src, dst, rs_s.at[E, way, s], rs_r.at[E, way, s], at_z(sign))

    def pipe_copy(q):
        return remote(
            outs.at[q], out.at[0, :, pl.ds(pl.multiple_of(q * F, F), F)], pp_s.at[q], pp_r.at[q], {"pipe": (p + 1) % 8}
        )

    wide = tokens[0].astype(jnp.float32)
    mean_square = jnp.mean(wide * wide, axis=-1, keepdims=True)
    normed = (wide * lax.rsqrt(mean_square + 1e-06) * gain[...]).astype(jnp.bfloat16)
    for q in range(E):
        xb[q, 0] = normed[:, q * F : (q + 1) * F]
    xe[0, 0] = normed[:, E * F :]

    pl.semaphore_wait(barrier, 18)
    for way in (0, 1):
        z_copy(0, way, 1).start()
    early_copy().start()

    line = lax.broadcasted_iota(jnp.int32, (16 * NZ, 1), 0)
    kind = line % 16
    expert_of = 4 * (line // 16) + line % 4
    spread = (lax.broadcasted_iota(jnp.int32, (16 * NZ, router.shape[1]), 1) == expert_of).astype(jnp.bfloat16)
    tall_router = jnp.dot(spread, router[0], preferred_element_type=jnp.float32).astype(jnp.bfloat16)
    score = jax.nn.sigmoid(
        lax.dot_general(tall_router, normed, (((1,), (1,)), ((), ())), preferred_element_type=jnp.float32)
    )
    hit = jnp.zeros((16 * NZ, tok), jnp.float32)
    for k in range(routes.shape[0]):
        hit = hit + (routes[k] == expert_of).astype(jnp.float32)
    later = (
        lax.broadcasted_iota(jnp.int32, (tok, tok), 0) < lax.broadcasted_iota(jnp.int32, (tok, tok), 1)
    ).astype(jnp.bfloat16)
    rank = jnp.dot(hit.astype(jnp.bfloat16), later, preferred_element_type=jnp.float32)
    total = jnp.sum(jnp.where(kind < 4, hit * score, 0.0), axis=0, keepdims=True)
    gate = score / total
    packed = jnp.where(
        kind < 4, jnp.where(hit > 0.0, rank, FAR), jnp.where((kind < 8) & (hit > 0.0), gate, 0.0)
    )
    pts[...] = packed.astype(jnp.bfloat16).reshape(NZ, 16, tok)
    for d, col in pt_all:
        pt_copy(d, col).start()
    pt[0, 0] = pts[z]

    def of_chip(first, second):
        return jnp.where(a == 0, first, second)

    def build_sel():
        for d, col in pt_all:
            pt_copy(d, col).wait_recv()
        row = lax.broadcasted_iota(jnp.int32, (ROWS, tok), 0).astype(jnp.float32)
        for g in range(2):
            for i in range(GROUP):
                tile = pt[0, g * GROUP + i].astype(jnp.float32)
                for j in range(4):
                    same = (row - float(CAP * i)) == tile[j : j + 1, :]
                    sel[g, j * ROWS : (j + 1) * ROWS, i * tok : (i + 1) * tok] = jnp.where(same, 1.0, 0.0).astype(
                        jnp.bfloat16
                    )

    def build_sel_e():
        row = lax.broadcasted_iota(jnp.int32, (ROWS, tok), 0).astype(jnp.float32)
        for g in range(2):
            for i in range(GROUP):
                tile = pt[1, g * GROUP + i].astype(jnp.float32)
                for j in range(2):
                    same = (row - float(CAP * i)) == of_chip(tile[j : j + 1, :], tile[2 + j : 3 + j, :])
                    sel_e[g, j * ROWS : (j + 1) * ROWS, i * tok : (i + 1) * tok] = jnp.where(same, 1.0, 0.0).astype(
                        jnp.bfloat16
                    )

    def build_wmap(col):
        turned = jnp.transpose(pt[col].reshape(16 * NZ, tok).astype(jnp.float32))
        wide_place = lax.broadcasted_iota(jnp.int32, (tok, 4 * ROWS), 1).astype(jnp.float32)
        place = lax.broadcasted_iota(jnp.int32, (tok, 2 * ROWS), 1).astype(jnp.float32)
        for g in range(2):
            for i in range(GROUP):
                first = (g * GROUP + i) * 16
                rank_of = [turned[:, first + j : first + j + 1] for j in range(4)]
                gate_of = [turned[:, first + 4 + j : first + 5 + j] for j in range(4)]
                part = slice(i * tok, (i + 1) * tok)
                if col == 0:
                    value = jnp.zeros((tok, 4 * ROWS), jnp.float32)
                    for j in range(4):
                        value = jnp.where(wide_place == rank_of[j] + float(ROWS * j + CAP * i), gate_of[j], value)
                    wmap[g, part] = value.astype(jnp.bfloat16)
                value = jnp.zeros((tok, 2 * ROWS), jnp.float32)
                for j in range(2):
                    here = of_chip(rank_of[j], rank_of[2 + j]) + float(ROWS * j + CAP * i)
                    value = jnp.where(place == here, of_chip(gate_of[j], gate_of[2 + j]), value)
                wmap_e[col, g, part] = value.astype(jnp.bfloat16)

    def valid(q, body):
        @pl.when((q >= 0) & (q < E))
        def _():
            body(q)

    def forward(s):
        def body(q):
            for way in (0, 1):
                if s > 1:
                    z_copy(q, way, s - 1).wait_recv()
                z_copy(q, way, s).start()

        return body

    def forward_e(s):
        if s == 1:
            early_copy().wait_recv()
        for way in (0, 1):
            if s > 1:
                ze_copy(way, s - 1).wait_recv()
            ze_copy(way, s).start()

    def select(g):
        def body(q):
            if g == 1:
                for way in (0, 1):
                    z_copy(q, way, 4).wait_recv()
            block = xb[q, g * GROUP : (g + 1) * GROUP].reshape(GROUP * tok, F)
            picked = jnp.dot(sel[g], block, preferred_element_type=jnp.float32).astype(jnp.bfloat16)
            for j in range(4):
                so[q, j, g] = picked[j * ROWS : (j + 1) * ROWS]
            for t in (2, 3, 1):
                x_copy(q, t, g).start()
            x_own(q, g).start()

        return body

    def select_e():
        for way in (0, 1):
            ze_copy(way, 4).wait_recv()
        here = pl.ds(pl.multiple_of(a * 2 * ROWS, 2 * ROWS), 2 * ROWS)
        for g in range(2):
            for col in (0, 1):
                block = xe[col, g * GROUP : (g + 1) * GROUP].reshape(GROUP * tok, F)
                chosen = sel_e[g] if col else sel[g, here]
                picked = jnp.dot(chosen, block, preferred_element_type=jnp.float32).astype(jnp.bfloat16)
                source = 1 - a if col else a
                for j in range(2):
                    so[E, 2 * j + source, g] = picked[j * ROWS : (j + 1) * ROWS]
        xe_copy().start()
        xe_own().start()

    def multiply(q):
        rows = xs[q].reshape(8 * ROWS, F)
        part = pl.ds(pl.multiple_of(q * F, F), F)
        acc_g[...] += jnp.dot(rows, wg[part], preferred_element_type=jnp.float32)
        acc_u[...] += jnp.dot(rows, wu[part], preferred_element_type=jnp.float32)

    def receive(q):
        for g in (0, 1):
            for t in (1, 2, 3):
                x_copy(q, t, g).wait_recv()
            x_own(q, g).wait()

    LAG = 3

    def gather_tick(tau, carry):
        valid(tau - 4, select(1))
        for s in (4, 3, 2, 1):
            if s > 1:
                valid(tau - s + 1, forward(s))
            else:

                @pl.when((tau > 0) & (tau < E))
                def _():
                    forward(1)(tau)

            @pl.when(tau - s + 1 == E)
            def _():
                forward_e(s)

        @pl.when(tau - 4 == E)
        def _():
            select_e()

        valid(tau - 2, select(0))

        def take(q):
            receive(q)
            multiply(q)

        @pl.when(tau < E + 5)
        def _():
            valid(tau - 4 - LAG, take)

        @pl.when(tau == E + 5)
        def _():
            xe_copy().wait_recv()
            xe_own().wait()
            multiply(E)

        @pl.when(tau > E + 5)
        def _():
            valid(tau - 5 - LAG, take)

        return carry

    lax.fori_loop(0, 2, gather_tick, 0)
    build_sel()
    lax.fori_loop(2, 4, gather_tick, 0)
    acc_g[...] = jnp.zeros_like(acc_g)
    acc_u[...] = jnp.zeros_like(acc_u)
    for w_copy in w_copies:
        w_copy.wait()
    build_sel_e()
    lax.fori_loop(4, 6, gather_tick, 0)
    build_wmap(0)
    lax.fori_loop(6, 7, gather_tick, 0)
    build_wmap(1)
    lax.fori_loop(7, nq + 4 + LAG, gather_tick, 0)

    def sent(q, carry):
        for g in (0, 1):
            for t in (1, 2, 3):
                x_copy(q, t, g).wait_send()
        return carry

    lax.fori_loop(0, E, sent, 0)
    xe_copy().wait_send()

    def act(t):
        for h in (0, 1):
            part = pl.ds(pl.multiple_of((2 * level[t] + h) * ROWS, ROWS), ROWS)
            v = acc_g[part]
            hid[part] = (v / (1.0 + jnp.exp(-v)) * acc_u[part]).astype(jnp.bfloat16)

    def produce_for(q, t):
        rows = pl.ds(pl.multiple_of(2 * level[t] * ROWS, 2 * ROWS), 2 * ROWS)
        part = pl.ds(pl.multiple_of(q * F, F), F)
        y = jnp.dot(hid[rows], wd[:, part], preferred_element_type=jnp.float32).astype(jnp.bfloat16)
        for g in (1, 0):
            so[q, level[t], g] = y[g * ROWS : (g + 1) * ROWS]

    def product(q):
        part = pl.ds(pl.multiple_of(q * F, F), F)
        return jnp.dot(hid[...], wd[:, part], preferred_element_type=jnp.float32).astype(jnp.bfloat16)

    def produce(q):
        y = product(q)
        for k in range(4):
            for g in range(2):
                n = (2 * k + g) * ROWS
                so[q, k, g] = y[n : n + ROWS]
        for g in (1, 0):
            for t in (2, 3, 1):
                y_copy(q, t, g).start()
            y_own(q, g).start()

    def produce_e():
        y = product(E)
        for s in range(2):
            for j in range(2):
                for g in range(2):
                    n = ((2 * s + j) * 2 + g) * ROWS
                    so[E, 2 * j + s, g] = y[n : n + ROWS]
        ye_copy().start()
        ye_own().start()

    def unselect(g):
        def body(q):
            for t in (1, 2, 3):
                y_copy(q, t, g).wait_recv()
            y_own(q, g).wait()
            rows = yr[q, g].reshape(4 * ROWS, F)
            sums = jnp.dot(wmap[g], rows, preferred_element_type=jnp.float32)
            for i in range(GROUP):
                block = sums[i * tok : (i + 1) * tok]
                if g * GROUP + i == 7:
                    for way in (0, 1):
                        part = slice(way * half, (way + 1) * half)
                        rss[q, way, 0, part] = block[part].astype(jnp.bfloat16)
                else:
                    cb[q % KEPT, g * GROUP + i] = block
            if g == 1:
                for way in (0, 1):
                    rs_copy(q, way, 0).start()

        return body

    def unselect_e():
        ye_copy().wait_recv()
        ye_own().wait()
        for g in (1, 0):
            for col in (0, 1):
                source = 1 - a if col else a
                rows = yr_e[source, g].reshape(2 * ROWS, F)
                sums = jnp.dot(wmap_e[col, g], rows, preferred_element_type=jnp.float32)
                for i in range(GROUP):
                    block = sums[i * tok : (i + 1) * tok]
                    if g * GROUP + i == 7:
                        for way in (0, 1):
                            part = slice(way * half, (way + 1) * half)
                            rss_e[way, 0, col, part] = block[part].astype(jnp.bfloat16)
                    else:
                        cb_e[col, g * GROUP + i] = block
            if g == 1:
                for way in (0, 1):
                    rse_copy(way, 0).start()

    def step(own, came, sent_on, way, s):
        if s == 1:
            add, keep = slice(way * half, (way + 1) * half), slice((1 - way) * half, (2 - way) * half)
            sent_on[add] = (own[add] + came[add].astype(jnp.float32)).astype(jnp.bfloat16)
            sent_on[keep] = own[keep].astype(jnp.bfloat16)
        else:
            sent_on[...] = (own[...] + came[...].astype(jnp.float32)).astype(jnp.bfloat16)

    def pass_on(s):
        def body(q):
            for way in (0, 1):
                rs_copy(q, way, s - 1).wait_recv()
                slot = SLOT[(4 - s) * (1 - 2 * way)]
                step(cb.at[q % KEPT, slot], rsr.at[q, way, s - 1], rss.at[q, way, s], way, s)
                rs_copy(q, way, s).start()

        return body

    def pass_on_e(s):
        for way in (0, 1):
            rse_copy(way, s - 1).wait_recv()
            slot = SLOT[(4 - s) * (1 - 2 * way)]
            for col in (0, 1):
                step(cb_e.at[col, slot], rsr_e.at[way, s - 1, col], rss_e.at[way, s, col], way, s)
            rse_copy(way, s).start()

    def finish(q):
        for way in (0, 1):
            rs_copy(q, way, 3).wait_recv()
        part = pl.ds(pl.multiple_of(q * F, F), F)
        moe = cb[q % KEPT, 0] + rsr[q, 0, 3].astype(jnp.float32) + rsr[q, 1, 3].astype(jnp.float32)
        outs[q] = (tokens[0, :, part].astype(jnp.float32) + moe).astype(jnp.bfloat16)
        pipe_copy(q).start()

    def cross_e():
        for way in (0, 1):
            rse_copy(way, 3).wait_recv()
        for col in (0, 1):
            total = cb_e[col, 0] + rsr_e[0, 3, col].astype(jnp.float32) + rsr_e[1, 3, col].astype(jnp.float32)
            if col:
                last[0] = total.astype(jnp.bfloat16)
            else:
                cb_e[0, 0] = total
        late_copy().start()

    def finish_e():
        late_copy().wait_recv()
        moe = cb_e[0, 0] + last[1].astype(jnp.float32)
        outs[E] = (tokens[0, :, E * F :].astype(jnp.float32) + moe).astype(jnp.bfloat16)
        pipe_copy(E).start()

    for t in (2, 3, 1, 0):
        act(t)
        produce_for(0, t)
        for g in (1, 0):
            if t:
                y_copy(0, t, g).start()
            else:
                y_own(0, g).start()
    produce_e()
    unselect_e()
    LEAD = 2
    for q in range(1, LEAD):
        produce(q)

    def combine_tick(tau, carry):
        valid(tau - 1, pass_on(2))
        for s in (1, 2, 3):

            @pl.when(tau == s - 1)
            def _():
                pass_on_e(s)

        @pl.when(tau == 3)
        def _():
            cross_e()

        @pl.when(tau == 4)
        def _():
            finish_e()

        valid(tau - 2, finish)
        valid(tau, unselect(1))
        valid(tau - 1, pass_on(3))

        @pl.when(tau + LEAD < E)
        def _():
            produce(tau + LEAD)

        @pl.when(tau < E)
        def _():
            pass_on(1)(tau)
            unselect(0)(tau)

        return carry

    lax.fori_loop(0, E + 2, combine_tick, 0)

    def drain(q, carry):
        for way in (0, 1):
            for s in range(1, 5):
                z_copy(q, way, s).wait_send()
            for s in range(4):
                rs_copy(q, way, s).wait_send()
        for g in (0, 1):
            for t in (1, 2, 3):
                y_copy(q, t, g).wait_send()
        pipe_copy(q).wait()
        return carry

    for d, col in pt_all:
        pt_copy(d, col).wait_send()
    for way in (0, 1):
        for s in range(1, 5):
            ze_copy(way, s).wait_send()
        for s in range(4):
            rse_copy(way, s).wait_send()
    early_copy().wait_send()
    late_copy().wait_send()
    ye_copy().wait_send()
    lax.fori_loop(0, E, drain, 0)
    pipe_copy(E).wait()


def local(tokens, routes, norm_gain, router_weight, w_gate, w_up, w_down):
    tok, width = tokens.shape[1:]
    ff = w_gate.shape[3]
    nq = 8
    F = width // nq
    bf, f32 = jnp.bfloat16, jnp.float32
    vmem = pl.BlockSpec(memory_space=pltpu.VMEM)
    anywhere = pl.BlockSpec(memory_space=pl.ANY)
    dma = pltpu.SemaphoreType.DMA
    return pl.pallas_call(
        functools.partial(kernel, nq),
        out_shape=jax.ShapeDtypeStruct(tokens.shape, bf),
        in_specs=[vmem, vmem, vmem, vmem, anywhere, anywhere, anywhere],
        out_specs=anywhere,
        scratch_shapes=[
            pltpu.VMEM((nq - 1, NZ, tok, F), bf),
            pltpu.VMEM((2, NZ, tok, F), bf),
            pltpu.VMEM((NZ, 16, tok), bf),
            pltpu.VMEM((2, NZ, 16, tok), bf),
            pltpu.VMEM((2, 4 * ROWS, GROUP * tok), bf),
            pltpu.VMEM((2, GROUP * tok, 4 * ROWS), bf),
            pltpu.VMEM((2, 2 * ROWS, GROUP * tok), bf),
            pltpu.VMEM((2, 2, GROUP * tok, 2 * ROWS), bf),
            pltpu.VMEM((nq, 4, 2, ROWS, F), bf),
            pltpu.VMEM((nq, 2, 2, 2, ROWS, F), bf),
            pltpu.VMEM((nq - 1, 2, 4, ROWS, F), bf),
            pltpu.VMEM((2, 2, 2, ROWS, F), bf),
            pltpu.VMEM((8 * ROWS, ff), f32),
            pltpu.VMEM((8 * ROWS, ff), f32),
            pltpu.VMEM((8 * ROWS, ff), bf),
            pltpu.VMEM((KEPT, 7, tok, F), f32),
            pltpu.VMEM((2, 7, tok, F), f32),
            pltpu.VMEM((nq - 1, 2, 4, tok, F), bf),
            pltpu.VMEM((nq - 1, 2, 4, tok, F), bf),
            pltpu.VMEM((2, 4, 2, tok, F), bf),
            pltpu.VMEM((2, 4, 2, tok, F), bf),
            pltpu.VMEM((2, tok, F), bf),
            pltpu.VMEM((nq, tok, F), bf),
            pltpu.VMEM((width, ff), bf),
            pltpu.VMEM((width, ff), bf),
            pltpu.VMEM((ff, width), bf),
            dma((nq, 2, 4)),
            dma((nq, 2, 4)),
            dma((2, NZ)),
            dma((2, NZ)),
            dma((nq, 4, 2)),
            dma((nq, 4, 2)),
            dma((nq, 4, 2)),
            dma((nq, 4, 2)),
            dma((nq, 2, 4)),
            dma((nq, 2, 4)),
            dma((2,)),
            dma((2,)),
            dma((nq,)),
            dma((nq,)),
            dma((3,)),
        ],
        compiler_params=pltpu.CompilerParams(
            collective_id=0, has_side_effects=True, vmem_limit_bytes=62 * 2**20
        ),
        name="relay_moe",
    )(tokens, jnp.transpose(routes, (2, 0, 1)), norm_gain, jnp.swapaxes(router_weight, 1, 2), w_gate, w_up, w_down)


def solution(mesh):
    return jax.shard_map(
        local,
        mesh=mesh,
        in_specs=(
            P("pipe", "expert", None),
            P("pipe", "expert", None),
            P("pipe", None),
            P("pipe", None, None),
            P("pipe", "expert", None, None),
            P("pipe", "expert", None, None),
            P("pipe", "expert", None, None),
        ),
        out_specs=P("pipe", "expert", None),
        check_vma=False,
    )
```

time: 167 us -> 164 us (0.982)
  local copies, waits for them, and re-layouts: 5.2 us -> 1.88 us
    unnamed x3 -> x1, local copies, waits for them, and re-layouts: 5.2 us -> 1.88 us
where the time goes in v2:
time: 164 us
  Pallas kernels  162 us (99%)
  local copies, waits for them, and re-layouts  1.88 us (1%)
    pallas_call x1, Pallas kernels, local(): pl.pallas_call(functools.partial(kernel, nq), out_shape=jax.ShapeDtypeStr...  162 us

profile of v2, /device:TPU:2, one launch (start us, length us, event | category | flops | bytes accessed | tf_op | source)
XLA Modules:
  0.0 163.6 jit_solution(16031753230495244008)
XLA Ops:
  0.0 161.7 %relay_moe.1 = bf16[1,128,2048]{2,1,0:T(8,128)(2,1)} custom-call(bf16[1,128,2048]{2,1,0:T(8,128)(2,1)} %tokens.1, s32[6,1,128]{2,1,0:T(1,128)} %bitcast.3, f32[1,2048]{1,0:T(1,128)} %gain.1, bf16[1,32,2048]{2,1,0:T(8,128)(2,1)} %bitcast.2, bf16[1,1,2048,768]{3,2,1,0:T(8,128)(2,1)} %wg_hbm.1, bf16[1,1,2048,768]{3,2,1,0:T(8,128)(2,1)} %wu_hbm.1, ...), custom_call_target="tpu_custom_call" | custom-call | tf_op jit(solution)/shard_map/relay_moe/pallas_call | solution.py:576
  161.7 1.9 %copy.9 = bf16[1,128,2048]{2,1,0:T(8,128)(2,1)} copy(bf16[1,128,2048]{2,1,0:T(8,128)(2,1)} %relay_moe.1) | data formatting | bytes 1048576

commit v3 on v2

--- a/solution.py
+++ b/solution.py
@@ -12,19 +12,20 @@
 CAP = 36
 GROUP = 4
 ROWS = GROUP * CAP
-KEPT = 4
+KEPT = 5
 FAR = 1024.0
 SLOT = {0: 0, -1: 1, 1: 2, -2: 3, 2: 4, -3: 5, 3: 6, 4: 7, -4: 7}
 
 
 def kernel(
-    nq, tokens, routes, gain, router, wg_hbm, wu_hbm, wd_hbm, out,
-    xb, xe, pts, pt, sel, wmap, sel_e, wmap_e, so, xs, yr, yr_e, acc_g, acc_u, hid, cb, cb_e, rss, rsr, rss_e, rsr_e,
+    nq, tok_hbm, routes, gain, router, wg_hbm, wu_hbm, wd_hbm, out,
+    tokens, xb, xe, own_rank, own_gate, pt_rank, pt_gate, sel, wmap, sel_e, wmap_e, so, xs, yr, yr_e, acc_g, acc_u, hid, cb, cb_e, rss, rsr, rss_e, rsr_e,
     last, outs, wg, wu, wd,
     zs_s, zs_r, pt_s, pt_r, xs_s, xs_r, ys_s, ys_r, rs_s, rs_r, ex_s, ex_r, pp_s, pp_r, w_sem,
 ):
-    width = tokens.shape[2]
-    tok = tokens.shape[1]
+    tok, width = tokens.shape
+    tok_copy = pltpu.make_async_copy(tok_hbm.at[0], tokens, w_sem.at[3])
+    tok_copy.start()
     half = tok // 2
     F = width // nq
     E = nq - 1
@@ -57,9 +58,6 @@
         pltpu.make_async_copy(wu_hbm.at[0, 0], wu, w_sem.at[1]),
         pltpu.make_async_copy(wd_hbm.at[0, 0], wd, w_sem.at[2]),
     ]
-    for w_copy in w_copies:
-        w_copy.start()
-
     def remote(src, dst, s_sem, r_sem, where):
         return pltpu.make_async_remote_copy(
             src_ref=src, dst_ref=dst, send_sem=s_sem, recv_sem=r_sem, device_id=where, device_id_type=MESH
@@ -81,10 +79,15 @@
             src, dst = src.at[:, part], dst.at[:, part]
         return remote(src, dst, zs_s.at[E, way, s - 1], zs_r.at[E, way, s - 1], at_z(sign))
 
-    def pt_copy(d, col):
+    def pt_copy(kind, d, col):
         n = SLOT[-d] if d else 0
+        mine_all, theirs = ((own_rank, pt_rank), (own_gate, pt_gate))[kind]
         return remote(
-            pts.at[(z + d + NZ) % NZ], pt.at[col, n], pt_s.at[col, n], pt_r.at[col, n], across(d) if col else at_z(d)
+            mine_all.at[(z + d + NZ) % NZ],
+            theirs.at[col, n],
+            pt_s.at[kind, col, n],
+            pt_r.at[kind, col, n],
+            across(d) if col else at_z(d),
         )
 
     pt_all = [(d, col) for d in (1, -1, 2, -2, 3, -3, 4, 0) for col in (0, 1) if d or col]
@@ -146,26 +149,8 @@
             outs.at[q], out.at[0, :, pl.ds(pl.multiple_of(q * F, F), F)], pp_s.at[q], pp_r.at[q], {"pipe": (p + 1) % 8}
         )
 
-    wide = tokens[0].astype(jnp.float32)
-    mean_square = jnp.mean(wide * wide, axis=-1, keepdims=True)
-    normed = (wide * lax.rsqrt(mean_square + 1e-06) * gain[...]).astype(jnp.bfloat16)
-    for q in range(E):
-        xb[q, 0] = normed[:, q * F : (q + 1) * F]
-    xe[0, 0] = normed[:, E * F :]
-
-    pl.semaphore_wait(barrier, 18)
-    for way in (0, 1):
-        z_copy(0, way, 1).start()
-    early_copy().start()
-
     line = lax.broadcasted_iota(jnp.int32, (16 * NZ, 1), 0)
-    kind = line % 16
     expert_of = 4 * (line // 16) + line % 4
-    spread = (lax.broadcasted_iota(jnp.int32, (16 * NZ, router.shape[1]), 1) == expert_of).astype(jnp.bfloat16)
-    tall_router = jnp.dot(spread, router[0], preferred_element_type=jnp.float32).astype(jnp.bfloat16)
-    score = jax.nn.sigmoid(
-        lax.dot_general(tall_router, normed, (((1,), (1,)), ((), ())), preferred_element_type=jnp.float32)
-    )
     hit = jnp.zeros((16 * NZ, tok), jnp.float32)
     for k in range(routes.shape[0]):
         hit = hit + (routes[k] == expert_of).astype(jnp.float32)
@@ -173,37 +158,59 @@
         lax.broadcasted_iota(jnp.int32, (tok, tok), 0) < lax.broadcasted_iota(jnp.int32, (tok, tok), 1)
     ).astype(jnp.bfloat16)
     rank = jnp.dot(hit.astype(jnp.bfloat16), later, preferred_element_type=jnp.float32)
-    total = jnp.sum(jnp.where(kind < 4, hit * score, 0.0), axis=0, keepdims=True)
-    gate = score / total
-    packed = jnp.where(
-        kind < 4, jnp.where(hit > 0.0, rank, FAR), jnp.where((kind < 8) & (hit > 0.0), gate, 0.0)
+    own_rank[...] = jnp.where(hit > 0.0, rank, FAR).astype(jnp.bfloat16).reshape(NZ, 16, tok)
+    pt_rank[0, 0] = own_rank[z]
+
+    tok_copy.wait()
+    wide = tokens[...].astype(jnp.float32)
+    mean_square = jnp.mean(wide * wide, axis=-1, keepdims=True)
+    normed = (wide * lax.rsqrt(mean_square + 1e-06) * gain[...]).astype(jnp.bfloat16)
+    for q in range(E):
+        xb[q, 0] = normed[:, q * F : (q + 1) * F]
+    xe[0, 0] = normed[:, E * F :]
+
+    pl.semaphore_wait(barrier, 18)
+    for way in (0, 1):
+        z_copy(0, way, 1).start()
+    for d, col in pt_all:
+        pt_copy(0, d, col).start()
+    early_copy().start()
+    for w_copy in w_copies:
+        w_copy.start()
+
+    spread = (lax.broadcasted_iota(jnp.int32, (16 * NZ, router.shape[1]), 1) == expert_of).astype(jnp.bfloat16)
+    tall_router = jnp.dot(spread, router[0], preferred_element_type=jnp.float32).astype(jnp.bfloat16)
+    score = jax.nn.sigmoid(
+        lax.dot_general(tall_router, normed, (((1,), (1,)), ((), ())), preferred_element_type=jnp.float32)
     )
-    pts[...] = packed.astype(jnp.bfloat16).reshape(NZ, 16, tok)
-    for d, col in pt_all:
-        pt_copy(d, col).start()
-    pt[0, 0] = pts[z]
+    total = jnp.sum(jnp.where(line % 16 < 4, hit * score, 0.0), axis=0, keepdims=True)
+    own_gate[...] = jnp.where(hit > 0.0, score / total, 0.0).astype(jnp.bfloat16).reshape(NZ, 16, tok)
+    pt_gate[0, 0] = own_gate[z]
 
     def of_chip(first, second):
         return jnp.where(a == 0, first, second)
 
-    def build_sel():
+    def build_sel(g):
         for d, col in pt_all:
-            pt_copy(d, col).wait_recv()
+            if SLOT[-d] // GROUP == g and not col:
+                pt_copy(0, d, col).wait_recv()
+        row = lax.broadcasted_iota(jnp.int32, (ROWS, tok), 0).astype(jnp.float32)
+        for i in range(GROUP):
+            tile = pt_rank[0, g * GROUP + i].astype(jnp.float32)
+            for j in range(4):
+                same = (row - float(CAP * i)) == tile[j : j + 1, :]
+                sel[g, j * ROWS : (j + 1) * ROWS, i * tok : (i + 1) * tok] = jnp.where(same, 1.0, 0.0).astype(
+                    jnp.bfloat16
+                )
+
+    def build_sel_e():
+        for d, col in pt_all:
+            if col:
+                pt_copy(0, d, col).wait_recv()
         row = lax.broadcasted_iota(jnp.int32, (ROWS, tok), 0).astype(jnp.float32)
         for g in range(2):
             for i in range(GROUP):
-                tile = pt[0, g * GROUP + i].astype(jnp.float32)
-                for j in range(4):
-                    same = (row - float(CAP * i)) == tile[j : j + 1, :]
-                    sel[g, j * ROWS : (j + 1) * ROWS, i * tok : (i + 1) * tok] = jnp.where(same, 1.0, 0.0).astype(
-                        jnp.bfloat16
-                    )
-
-    def build_sel_e():
-        row = lax.broadcasted_iota(jnp.int32, (ROWS, tok), 0).astype(jnp.float32)
-        for g in range(2):
-            for i in range(GROUP):
-                tile = pt[1, g * GROUP + i].astype(jnp.float32)
+                tile = pt_rank[1, g * GROUP + i].astype(jnp.float32)
                 for j in range(2):
                     same = (row - float(CAP * i)) == of_chip(tile[j : j + 1, :], tile[2 + j : 3 + j, :])
                     sel_e[g, j * ROWS : (j + 1) * ROWS, i * tok : (i + 1) * tok] = jnp.where(same, 1.0, 0.0).astype(
@@ -211,14 +218,19 @@
                     )
 
     def build_wmap(col):
-        turned = jnp.transpose(pt[col].reshape(16 * NZ, tok).astype(jnp.float32))
+        for d, side in pt_all:
+            if side == col:
+                pt_copy(1, d, col).wait_recv()
+        turned, turned_gate = [
+            jnp.transpose(table[col].reshape(16 * NZ, tok).astype(jnp.float32)) for table in (pt_rank, pt_gate)
+        ]
         wide_place = lax.broadcasted_iota(jnp.int32, (tok, 4 * ROWS), 1).astype(jnp.float32)
         place = lax.broadcasted_iota(jnp.int32, (tok, 2 * ROWS), 1).astype(jnp.float32)
         for g in range(2):
             for i in range(GROUP):
                 first = (g * GROUP + i) * 16
                 rank_of = [turned[:, first + j : first + j + 1] for j in range(4)]
-                gate_of = [turned[:, first + 4 + j : first + 5 + j] for j in range(4)]
+                gate_of = [turned_gate[:, first + j : first + j + 1] for j in range(4)]
                 part = slice(i * tok, (i + 1) * tok)
                 if col == 0:
                     value = jnp.zeros((tok, 4 * ROWS), jnp.float32)
@@ -338,19 +350,23 @@
 
         return carry
 
-    lax.fori_loop(0, 2, gather_tick, 0)
-    build_sel()
-    lax.fori_loop(2, 4, gather_tick, 0)
+    lax.fori_loop(1, 2, gather_tick, 0)
+    build_sel(0)
+    lax.fori_loop(2, 3, gather_tick, 0)
+    build_sel(1)
+    lax.fori_loop(3, 5, gather_tick, 0)
+    for d, col in pt_all:
+        pt_copy(1, d, col).start()
     acc_g[...] = jnp.zeros_like(acc_g)
     acc_u[...] = jnp.zeros_like(acc_u)
     for w_copy in w_copies:
         w_copy.wait()
     build_sel_e()
-    lax.fori_loop(4, 6, gather_tick, 0)
+    lax.fori_loop(5, 8, gather_tick, 0)
     build_wmap(0)
-    lax.fori_loop(6, 7, gather_tick, 0)
+    lax.fori_loop(8, 9, gather_tick, 0)
     build_wmap(1)
-    lax.fori_loop(7, nq + 4 + LAG, gather_tick, 0)
+    lax.fori_loop(9, nq + 4 + LAG, gather_tick, 0)
 
     def sent(q, carry):
         for g in (0, 1):
@@ -471,7 +487,7 @@
             rs_copy(q, way, 3).wait_recv()
         part = pl.ds(pl.multiple_of(q * F, F), F)
         moe = cb[q % KEPT, 0] + rsr[q, 0, 3].astype(jnp.float32) + rsr[q, 1, 3].astype(jnp.float32)
-        outs[q] = (tokens[0, :, part].astype(jnp.float32) + moe).astype(jnp.bfloat16)
+        outs[q] = (tokens[:, part].astype(jnp.float32) + moe).astype(jnp.bfloat16)
         pipe_copy(q).start()
 
     def cross_e():
@@ -488,7 +504,7 @@
     def finish_e():
         late_copy().wait_recv()
         moe = cb_e[0, 0] + last[1].astype(jnp.float32)
-        outs[E] = (tokens[0, :, E * F :].astype(jnp.float32) + moe).astype(jnp.bfloat16)
+        outs[E] = (tokens[:, E * F :].astype(jnp.float32) + moe).astype(jnp.bfloat16)
         pipe_copy(E).start()
 
     for t in (2, 3, 1, 0):
@@ -501,12 +517,27 @@
                 y_own(0, g).start()
     produce_e()
     unselect_e()
-    LEAD = 2
+    LEAD = 3
     for q in range(1, LEAD):
         produce(q)
 
+    def span(tau, s, body):
+        def one(q, carry):
+            body(q)
+            return carry
+
+        high = jnp.where(tau == E - 2 + s, E, jnp.minimum(tau - s + 1, E - 1))
+        lax.fori_loop(jnp.maximum(tau - s, 0), high, one, 0)
+
     def combine_tick(tau, carry):
-        valid(tau - 1, pass_on(2))
+        span(tau, 4, finish)
+        span(tau, 3, pass_on(3))
+        span(tau, 2, pass_on(2))
+
+        @pl.when((tau >= 1) & (tau < E))
+        def _():
+            pass_on(1)(tau - 1)
+
         for s in (1, 2, 3):
 
             @pl.when(tau == s - 1)
@@ -517,26 +548,25 @@
         def _():
             cross_e()
 
-        @pl.when(tau == 4)
+        @pl.when(tau == 5)
         def _():
             finish_e()
 
-        valid(tau - 2, finish)
         valid(tau, unselect(1))
-        valid(tau - 1, pass_on(3))
 
         @pl.when(tau + LEAD < E)
         def _():
             produce(tau + LEAD)
 
-        @pl.when(tau < E)
+        valid(tau, unselect(0))
+
+        @pl.when(tau == E - 1)
         def _():
             pass_on(1)(tau)
-            unselect(0)(tau)
 
         return carry
 
-    lax.fori_loop(0, E + 2, combine_tick, 0)
+    lax.fori_loop(0, E + 3, combine_tick, 0)
 
     def drain(q, carry):
         for way in (0, 1):
@@ -551,7 +581,8 @@
         return carry
 
     for d, col in pt_all:
-        pt_copy(d, col).wait_send()
+        for kind in (0, 1):
+            pt_copy(kind, d, col).wait_send()
     for way in (0, 1):
         for s in range(1, 5):
             ze_copy(way, s).wait_send()
@@ -576,12 +607,15 @@
     return pl.pallas_call(
         functools.partial(kernel, nq),
         out_shape=jax.ShapeDtypeStruct(tokens.shape, bf),
-        in_specs=[vmem, vmem, vmem, vmem, anywhere, anywhere, anywhere],
+        in_specs=[anywhere, vmem, vmem, vmem, anywhere, anywhere, anywhere],
         out_specs=anywhere,
         scratch_shapes=[
+            pltpu.VMEM((tok, width), bf),
             pltpu.VMEM((nq - 1, NZ, tok, F), bf),
             pltpu.VMEM((2, NZ, tok, F), bf),
             pltpu.VMEM((NZ, 16, tok), bf),
+            pltpu.VMEM((NZ, 16, tok), bf),
+            pltpu.VMEM((2, NZ, 16, tok), bf),
             pltpu.VMEM((2, NZ, 16, tok), bf),
             pltpu.VMEM((2, 4 * ROWS, GROUP * tok), bf),
             pltpu.VMEM((2, GROUP * tok, 4 * ROWS), bf),
@@ -607,8 +641,8 @@
             pltpu.VMEM((ff, width), bf),
             dma((nq, 2, 4)),
             dma((nq, 2, 4)),
-            dma((2, NZ)),
-            dma((2, NZ)),
+            dma((2, 2, NZ)),
+            dma((2, 2, NZ)),
             dma((nq, 4, 2)),
             dma((nq, 4, 2)),
             dma((nq, 4, 2)),
@@ -619,7 +653,7 @@
             dma((2,)),
             dma((nq,)),
             dma((nq,)),
-            dma((3,)),
+            dma((4,)),
         ],
         compiler_params=pltpu.CompilerParams(
             collective_id=0, has_side_effects=True, vmem_limit_bytes=62 * 2**20

time: 164 us -> 147 us (0.90)
  Pallas kernels: 162 us -> 144 us
    pallas_call x1, Pallas kernels: 162 us -> 144 us  [local(): pl.pallas_call(functools.partial(kernel, nq), out_shape=jax.ShapeDtypeStr...]
where the time goes in v3:
time: 147 us; the launch traced here: 146 us
  Pallas kernels  144 us (98%)
  local copies, waits for them, and re-layouts  1.88 us (1%)
    pallas_call x1, Pallas kernels, local(): pl.pallas_call(functools.partial(kernel, nq), out_shape=jax.ShapeDtypeStr...  144 us

profile of v3, /device:TPU:2, one launch (start us, length us, event | category | flops | bytes accessed | tf_op | source)
XLA Modules:
  0.0 146.0 jit_solution(11526171073444520057)
XLA Ops:
  0.0 144.1 %relay_moe.1 = bf16[1,128,2048]{2,1,0:T(8,128)(2,1)} custom-call(bf16[1,128,2048]{2,1,0:T(8,128)(2,1)} %tok_hbm.1, s32[6,1,128]{2,1,0:T(1,128)} %bitcast.3, f32[1,2048]{1,0:T(1,128)} %gain.1, bf16[1,32,2048]{2,1,0:T(8,128)(2,1)} %bitcast.2, bf16[1,1,2048,768]{3,2,1,0:T(8,128)(2,1)} %wg_hbm.1, bf16[1,1,2048,768]{3,2,1,0:T(8,128)(2,1)} %wu_hbm.1, ...), custom_call_target="tpu_custom_call" | custom-call | tf_op jit(solution)/shard_map/relay_moe/pallas_call | solution.py:607
  144.1 1.9 %copy.9 = bf16[1,128,2048]{2,1,0:T(8,128)(2,1)} copy(bf16[1,128,2048]{2,1,0:T(8,128)(2,1)} %relay_moe.1) | data formatting | bytes 1048576

commit v4 on v3

--- a/solution.py
+++ b/solution.py
@@ -12,14 +12,15 @@
 CAP = 36
 GROUP = 4
 ROWS = GROUP * CAP
-KEPT = 5
+NE = 1
+KEPT = 4
 FAR = 1024.0
 SLOT = {0: 0, -1: 1, 1: 2, -2: 3, 2: 4, -3: 5, 3: 6, 4: 7, -4: 7}
 
 
 def kernel(
     nq, tok_hbm, routes, gain, router, wg_hbm, wu_hbm, wd_hbm, out,
-    tokens, xb, xe, own_rank, own_gate, pt_rank, pt_gate, sel, wmap, sel_e, wmap_e, so, xs, yr, yr_e, acc_g, acc_u, hid, cb, cb_e, rss, rsr, rss_e, rsr_e,
+    tokens, xb, xe, own_rank, own_gate, pt_rank, pt_gate, sel, wmap, sel_e, wmap_e, so, xs, yr, yr_e, acc_g, acc_u, hid, cb, cb_e, rsr, rsr_e,
     last, outs, wg, wu, wd,
     zs_s, zs_r, pt_s, pt_r, xs_s, xs_r, ys_s, ys_r, rs_s, rs_r, ex_s, ex_r, pp_s, pp_r, w_sem,
 ):
@@ -28,7 +29,7 @@
     tok_copy.start()
     half = tok // 2
     F = width // nq
-    E = nq - 1
+    E = nq - NE
     p = lax.axis_index("pipe")
     e = lax.axis_index("expert")
     z, a, c = e // 4, (e // 2) % 2, e % 2
@@ -37,9 +38,6 @@
     def at_z(d):
         return {"expert": ((z + d + NZ) % NZ) * 4 + mine}
 
-    def across(d):
-        return {"expert": ((z + d + NZ) % NZ) * 4 + 2 * (1 - a) + c}
-
     level = [mine, 2 * a + (1 - c), 2 * (1 - a) + c, 2 * (1 - a) + (1 - c)]
 
     def at_level(t):
@@ -48,7 +46,6 @@
     barrier = pltpu.get_barrier_semaphore()
     for d in range(1, NZ):
         pl.semaphore_signal(barrier, inc=1, device_id=at_z(d), device_id_type=MESH)
-        pl.semaphore_signal(barrier, inc=1, device_id=across(d), device_id_type=MESH)
     for t in (1, 2, 3):
         pl.semaphore_signal(barrier, inc=1, device_id=at_level(t), device_id_type=MESH)
     pl.semaphore_signal(barrier, inc=1, device_id={"pipe": (p + 7) % 8}, device_id_type=MESH)
@@ -71,26 +68,26 @@
             src, dst = src.at[part], dst.at[part]
         return remote(src, dst, zs_s.at[q, way, s - 1], zs_r.at[q, way, s - 1], at_z(sign))
 
-    def ze_copy(way, s):
+    def ze_copy(i, way, s):
         sign = 1 - 2 * way
-        src, dst = xe.at[:, SLOT[-(s - 1) * sign]], xe.at[:, SLOT[-s * sign]]
+        src, dst = xe.at[i, :, SLOT[-(s - 1) * sign]], xe.at[i, :, SLOT[-s * sign]]
         if s == 4:
             part = pl.ds(way * half, half)
             src, dst = src.at[:, part], dst.at[:, part]
-        return remote(src, dst, zs_s.at[E, way, s - 1], zs_r.at[E, way, s - 1], at_z(sign))
-
-    def pt_copy(kind, d, col):
-        n = SLOT[-d] if d else 0
+        return remote(src, dst, zs_s.at[E + i, way, s - 1], zs_r.at[E + i, way, s - 1], at_z(sign))
+
+    def pt_copy(kind, d):
+        n = SLOT[-d]
         mine_all, theirs = ((own_rank, pt_rank), (own_gate, pt_gate))[kind]
         return remote(
-            mine_all.at[(z + d + NZ) % NZ],
-            theirs.at[col, n],
-            pt_s.at[kind, col, n],
-            pt_r.at[kind, col, n],
-            across(d) if col else at_z(d),
+            mine_all.at[(z + d + NZ) % NZ], theirs.at[0, n], pt_s.at[kind, 0, n], pt_r.at[kind, 0, n], at_z(d)
         )
 
-    pt_all = [(d, col) for d in (1, -1, 2, -2, 3, -3, 4, 0) for col in (0, 1) if d or col]
+    def pt_share(kind):
+        table = (pt_rank, pt_gate)[kind]
+        return remote(table.at[0], table.at[1], pt_s.at[kind, 1, 0], pt_r.at[kind, 1, 0], at_level(2))
+
+    pt_all = (1, -1, 2, -2, 3, -3, 4)
 
     def x_copy(q, t, g):
         return remote(
@@ -100,13 +97,12 @@
     def x_own(q, g):
         return pltpu.make_async_copy(so.at[q, mine, g], xs.at[q, a, c, g], xs_r.at[q, 0, g])
 
-    def xe_copy():
-        return remote(
-            so.at[E, pl.ds(2 * (1 - c), 2)], xs.at[E, :, c], xs_s.at[E, 1, 0], xs_r.at[E, 1, 0], at_level(1)
-        )
-
-    def xe_own():
-        return pltpu.make_async_copy(so.at[E, pl.ds(2 * c, 2)], xs.at[E, :, c], xs_r.at[E, 0, 0])
+    def xe_copy(i):
+        part = so.at[E + i, pl.ds(2 * (1 - c), 2)]
+        return remote(part, xs.at[E + i, :, c], xs_s.at[E + i, 1, 0], xs_r.at[E + i, 1, 0], at_level(1))
+
+    def xe_own(i):
+        return pltpu.make_async_copy(so.at[E + i, pl.ds(2 * c, 2)], xs.at[E + i, :, c], xs_r.at[E + i, 0, 0])
 
     def y_copy(q, t, g):
         return remote(so.at[q, level[t], g], yr.at[q, g, mine], ys_s.at[q, t, g], ys_r.at[q, t, g], at_level(t))
@@ -114,35 +110,34 @@
     def y_own(q, g):
         return pltpu.make_async_copy(so.at[q, mine, g], yr.at[q, g, mine], ys_r.at[q, 0, g])
 
-    def ye_copy():
-        return remote(
-            so.at[E, pl.ds(2 * (1 - c), 2)], yr_e.at[:, :, c], ys_s.at[E, 1, 0], ys_r.at[E, 1, 0], at_level(1)
-        )
-
-    def ye_own():
-        return pltpu.make_async_copy(so.at[E, pl.ds(2 * c, 2)], yr_e.at[:, :, c], ys_r.at[E, 0, 0])
-
-    def early_copy():
-        return remote(xe.at[0, 0], xe.at[1, 0], ex_s.at[0], ex_r.at[0], at_level(2))
-
-    def late_copy():
-        return remote(last.at[0], last.at[1], ex_s.at[1], ex_r.at[1], at_level(2))
+    def ye_copy(i):
+        part = so.at[E + i, pl.ds(2 * (1 - c), 2)]
+        return remote(part, yr_e.at[i, :, :, c], ys_s.at[E + i, 1, 0], ys_r.at[E + i, 1, 0], at_level(1))
+
+    def ye_own(i):
+        return pltpu.make_async_copy(so.at[E + i, pl.ds(2 * c, 2)], yr_e.at[i, :, :, c], ys_r.at[E + i, 0, 0])
+
+    def early_copy(i):
+        return remote(xe.at[i, 0, 0], xe.at[i, 1, 0], ex_s.at[i, 0], ex_r.at[i, 0], at_level(2))
+
+    def late_copy(i):
+        return remote(last.at[i, 0], last.at[i, 1], ex_s.at[i, 1], ex_r.at[i, 1], at_level(2))
 
     def rs_copy(q, way, s):
         sign = 1 - 2 * way
-        src, dst = rss.at[q, way, s], rsr.at[q, way, s]
+        src, dst = xb.at[q, way * 4 + s], rsr.at[q, way, s]
         if s == 0:
             part = pl.ds(way * half, half)
             src, dst = src.at[part], dst.at[part]
         return remote(src, dst, rs_s.at[q, way, s], rs_r.at[q, way, s], at_z(sign))
 
-    def rse_copy(way, s):
+    def rse_copy(i, way, s):
         sign = 1 - 2 * way
-        src, dst = rss_e.at[way, s], rsr_e.at[way, s]
+        src, dst = xe.at[i, :, way * 4 + s], rsr_e.at[i, way, s]
         if s == 0:
             part = pl.ds(way * half, half)
             src, dst = src.at[:, part], dst.at[:, part]
-        return remote(src, dst, rs_s.at[E, way, s], rs_r.at[E, way, s], at_z(sign))
+        return remote(src, dst, rs_s.at[E + i, way, s], rs_r.at[E + i, way, s], at_z(sign))
 
     def pipe_copy(q):
         return remote(
@@ -167,14 +162,16 @@
     normed = (wide * lax.rsqrt(mean_square + 1e-06) * gain[...]).astype(jnp.bfloat16)
     for q in range(E):
         xb[q, 0] = normed[:, q * F : (q + 1) * F]
-    xe[0, 0] = normed[:, E * F :]
-
-    pl.semaphore_wait(barrier, 18)
+    for i in range(NE):
+        xe[i, 0, 0] = normed[:, (E + i) * F : (E + i + 1) * F]
+
+    pl.semaphore_wait(barrier, 11)
     for way in (0, 1):
         z_copy(0, way, 1).start()
-    for d, col in pt_all:
-        pt_copy(0, d, col).start()
-    early_copy().start()
+    for d in pt_all:
+        pt_copy(0, d).start()
+    for i in range(NE):
+        early_copy(i).start()
     for w_copy in w_copies:
         w_copy.start()
 
@@ -191,9 +188,9 @@
         return jnp.where(a == 0, first, second)
 
     def build_sel(g):
-        for d, col in pt_all:
-            if SLOT[-d] // GROUP == g and not col:
-                pt_copy(0, d, col).wait_recv()
+        for d in pt_all:
+            if SLOT[-d] // GROUP == g:
+                pt_copy(0, d).wait_recv()
         row = lax.broadcasted_iota(jnp.int32, (ROWS, tok), 0).astype(jnp.float32)
         for i in range(GROUP):
             tile = pt_rank[0, g * GROUP + i].astype(jnp.float32)
@@ -204,9 +201,7 @@
                 )
 
     def build_sel_e():
-        for d, col in pt_all:
-            if col:
-                pt_copy(0, d, col).wait_recv()
+        pt_share(0).wait_recv()
         row = lax.broadcasted_iota(jnp.int32, (ROWS, tok), 0).astype(jnp.float32)
         for g in range(2):
             for i in range(GROUP):
@@ -218,9 +213,12 @@
                     )
 
     def build_wmap(col):
-        for d, side in pt_all:
-            if side == col:
-                pt_copy(1, d, col).wait_recv()
+        if col == 0:
+            for d in pt_all:
+                pt_copy(1, d).wait_recv()
+            pt_share(1).start()
+        else:
+            pt_share(1).wait_recv()
         turned, turned_gate = [
             jnp.transpose(table[col].reshape(16 * NZ, tok).astype(jnp.float32)) for table in (pt_rank, pt_gate)
         ]
@@ -257,13 +255,13 @@
 
         return body
 
-    def forward_e(s):
+    def forward_e(i, s):
         if s == 1:
-            early_copy().wait_recv()
+            early_copy(i).wait_recv()
         for way in (0, 1):
             if s > 1:
-                ze_copy(way, s - 1).wait_recv()
-            ze_copy(way, s).start()
+                ze_copy(i, way, s - 1).wait_recv()
+            ze_copy(i, way, s).start()
 
     def select(g):
         def body(q):
@@ -280,20 +278,20 @@
 
         return body
 
-    def select_e():
-        for way in (0, 1):
-            ze_copy(way, 4).wait_recv()
+    def select_e(i):
+        for way in (0, 1):
+            ze_copy(i, way, 4).wait_recv()
         here = pl.ds(pl.multiple_of(a * 2 * ROWS, 2 * ROWS), 2 * ROWS)
         for g in range(2):
             for col in (0, 1):
-                block = xe[col, g * GROUP : (g + 1) * GROUP].reshape(GROUP * tok, F)
+                block = xe[i, col, g * GROUP : (g + 1) * GROUP].reshape(GROUP * tok, F)
                 chosen = sel_e[g] if col else sel[g, here]
                 picked = jnp.dot(chosen, block, preferred_element_type=jnp.float32).astype(jnp.bfloat16)
                 source = 1 - a if col else a
                 for j in range(2):
-                    so[E, 2 * j + source, g] = picked[j * ROWS : (j + 1) * ROWS]
-        xe_copy().start()
-        xe_own().start()
+                    so[E + i, 2 * j + source, g] = picked[j * ROWS : (j + 1) * ROWS]
+        xe_copy(i).start()
+        xe_own(i).start()
 
     def multiply(q):
         rows = xs[q].reshape(8 * ROWS, F)
@@ -310,7 +308,6 @@
     LAG = 3
 
     def gather_tick(tau, carry):
-        valid(tau - 4, select(1))
         for s in (4, 3, 2, 1):
             if s > 1:
                 valid(tau - s + 1, forward(s))
@@ -320,33 +317,33 @@
                 def _():
                     forward(1)(tau)
 
-            @pl.when(tau - s + 1 == E)
+            @pl.when((tau - s + 1 >= E) & (tau - s + 1 < nq))
             def _():
-                forward_e(s)
-
-        @pl.when(tau - 4 == E)
-        def _():
-            select_e()
-
-        valid(tau - 2, select(0))
+                forward_e(tau - s + 1 - E, s)
+
+            if s == 3:
+                valid(tau - 2, select(0))
+
+        valid(tau - 4, select(1))
+
+        @pl.when((tau - 4 >= E) & (tau - 4 < nq))
+        def _():
+            select_e(tau - 4 - E)
+
 
         def take(q):
             receive(q)
             multiply(q)
 
-        @pl.when(tau < E + 5)
-        def _():
-            valid(tau - 4 - LAG, take)
-
-        @pl.when(tau == E + 5)
-        def _():
-            xe_copy().wait_recv()
-            xe_own().wait()
-            multiply(E)
-
-        @pl.when(tau > E + 5)
-        def _():
-            valid(tau - 5 - LAG, take)
+        @pl.when((tau - 4 - LAG >= 0) & (tau - 4 - LAG < E - 1))
+        def _():
+            take(tau - 4 - LAG)
+
+        @pl.when((tau - 5 >= E) & (tau - 5 < nq))
+        def _():
+            xe_copy(tau - 5 - E).wait_recv()
+            xe_own(tau - 5 - E).wait()
+            multiply(tau - 5)
 
         return carry
 
@@ -354,34 +351,40 @@
     build_sel(0)
     lax.fori_loop(2, 3, gather_tick, 0)
     build_sel(1)
+    pt_share(0).start()
     lax.fori_loop(3, 5, gather_tick, 0)
-    for d, col in pt_all:
-        pt_copy(1, d, col).start()
+    for d in pt_all:
+        pt_copy(1, d).start()
     acc_g[...] = jnp.zeros_like(acc_g)
     acc_u[...] = jnp.zeros_like(acc_u)
     for w_copy in w_copies:
         w_copy.wait()
+    lax.fori_loop(5, 7, gather_tick, 0)
     build_sel_e()
-    lax.fori_loop(5, 8, gather_tick, 0)
+    lax.fori_loop(7, 8, gather_tick, 0)
     build_wmap(0)
     lax.fori_loop(8, 9, gather_tick, 0)
     build_wmap(1)
-    lax.fori_loop(9, nq + 4 + LAG, gather_tick, 0)
+    lax.fori_loop(9, max(nq + 5, E + 3 + LAG), gather_tick, 0)
 
     def sent(q, carry):
+        for way in (0, 1):
+            for s in range(1, 5):
+                z_copy(q, way, s).wait_send()
         for g in (0, 1):
             for t in (1, 2, 3):
                 x_copy(q, t, g).wait_send()
         return carry
 
-    lax.fori_loop(0, E, sent, 0)
-    xe_copy().wait_send()
+    sides = [(a, c), (a, 1 - c), (1 - a, c), (1 - a, 1 - c)]
 
     def act(t):
-        for h in (0, 1):
-            part = pl.ds(pl.multiple_of((2 * level[t] + h) * ROWS, ROWS), ROWS)
-            v = acc_g[part]
-            hid[part] = (v / (1.0 + jnp.exp(-v)) * acc_u[part]).astype(jnp.bfloat16)
+        part = pl.ds(pl.multiple_of(2 * level[t] * ROWS, 2 * ROWS), 2 * ROWS)
+        rows = xs[(E - 1, *sides[t])].reshape(2 * ROWS, F)
+        slab = slice((E - 1) * F, E * F)
+        v = acc_g[part] + jnp.dot(rows, wg[slab], preferred_element_type=jnp.float32)
+        u = acc_u[part] + jnp.dot(rows, wu[slab], preferred_element_type=jnp.float32)
+        hid[part] = (v / (1.0 + jnp.exp(-v)) * u).astype(jnp.bfloat16)
 
     def produce_for(q, t):
         rows = pl.ds(pl.multiple_of(2 * level[t] * ROWS, 2 * ROWS), 2 * ROWS)
@@ -400,20 +403,23 @@
             for g in range(2):
                 n = (2 * k + g) * ROWS
                 so[q, k, g] = y[n : n + ROWS]
-        for g in (1, 0):
-            for t in (2, 3, 1):
-                y_copy(q, t, g).start()
-            y_own(q, g).start()
-
-    def produce_e():
-        y = product(E)
+        give(q, 1)
+        give(q - 1, 0)
+
+    def give(q, g):
+        for t in (2, 3, 1):
+            y_copy(q, t, g).start()
+        y_own(q, g).start()
+
+    def produce_e(i):
+        y = product(E + i)
         for s in range(2):
             for j in range(2):
                 for g in range(2):
                     n = ((2 * s + j) * 2 + g) * ROWS
-                    so[E, 2 * j + s, g] = y[n : n + ROWS]
-        ye_copy().start()
-        ye_own().start()
+                    so[E + i, 2 * j + s, g] = y[n : n + ROWS]
+        ye_copy(i).start()
+        ye_own(i).start()
 
     def unselect(g):
         def body(q):
@@ -427,7 +433,7 @@
                 if g * GROUP + i == 7:
                     for way in (0, 1):
                         part = slice(way * half, (way + 1) * half)
-                        rss[q, way, 0, part] = block[part].astype(jnp.bfloat16)
+                        xb[q, way * 4, part] = block[part].astype(jnp.bfloat16)
                 else:
                     cb[q % KEPT, g * GROUP + i] = block
             if g == 1:
@@ -436,25 +442,25 @@
 
         return body
 
-    def unselect_e():
-        ye_copy().wait_recv()
-        ye_own().wait()
+    def unselect_e(i):
+        ye_copy(i).wait_recv()
+        ye_own(i).wait()
         for g in (1, 0):
             for col in (0, 1):
                 source = 1 - a if col else a
-                rows = yr_e[source, g].reshape(2 * ROWS, F)
+                rows = yr_e[i, source, g].reshape(2 * ROWS, F)
                 sums = jnp.dot(wmap_e[col, g], rows, preferred_element_type=jnp.float32)
-                for i in range(GROUP):
-                    block = sums[i * tok : (i + 1) * tok]
-                    if g * GROUP + i == 7:
+                for n in range(GROUP):
+                    block = sums[n * tok : (n + 1) * tok]
+                    if g * GROUP + n == 7:
                         for way in (0, 1):
                             part = slice(way * half, (way + 1) * half)
-                            rss_e[way, 0, col, part] = block[part].astype(jnp.bfloat16)
+                            xe[i, col, way * 4, part] = block[part].astype(jnp.bfloat16)
                     else:
-                        cb_e[col, g * GROUP + i] = block
+                        cb_e[i, col, g * GROUP + n] = block
             if g == 1:
                 for way in (0, 1):
-                    rse_copy(way, 0).start()
+                    rse_copy(i, way, 0).start()
 
     def step(own, came, sent_on, way, s):
         if s == 1:
@@ -469,18 +475,18 @@
             for way in (0, 1):
                 rs_copy(q, way, s - 1).wait_recv()
                 slot = SLOT[(4 - s) * (1 - 2 * way)]
-                step(cb.at[q % KEPT, slot], rsr.at[q, way, s - 1], rss.at[q, way, s], way, s)
+                step(cb.at[q % KEPT, slot], rsr.at[q, way, s - 1], xb.at[q, way * 4 + s], way, s)
                 rs_copy(q, way, s).start()
 
         return body
 
-    def pass_on_e(s):
-        for way in (0, 1):
-            rse_copy(way, s - 1).wait_recv()
+    def pass_on_e(i, s):
+        for way in (0, 1):
+            rse_copy(i, way, s - 1).wait_recv()
             slot = SLOT[(4 - s) * (1 - 2 * way)]
             for col in (0, 1):
-                step(cb_e.at[col, slot], rsr_e.at[way, s - 1, col], rss_e.at[way, s, col], way, s)
-            rse_copy(way, s).start()
+                step(cb_e.at[i, col, slot], rsr_e.at[i, way, s - 1, col], xe.at[i, col, way * 4 + s], way, s)
+            rse_copy(i, way, s).start()
 
     def finish(q):
         for way in (0, 1):
@@ -490,88 +496,110 @@
         outs[q] = (tokens[:, part].astype(jnp.float32) + moe).astype(jnp.bfloat16)
         pipe_copy(q).start()
 
-    def cross_e():
-        for way in (0, 1):
-            rse_copy(way, 3).wait_recv()
+    def cross_e(i):
+        for way in (0, 1):
+            rse_copy(i, way, 3).wait_recv()
         for col in (0, 1):
-            total = cb_e[col, 0] + rsr_e[0, 3, col].astype(jnp.float32) + rsr_e[1, 3, col].astype(jnp.float32)
+            total = cb_e[i, col, 0] + rsr_e[i, 0, 3, col].astype(jnp.float32) + rsr_e[i, 1, 3, col].astype(jnp.float32)
             if col:
-                last[0] = total.astype(jnp.bfloat16)
+                last[i, 0] = total.astype(jnp.bfloat16)
             else:
-                cb_e[0, 0] = total
-        late_copy().start()
-
-    def finish_e():
-        late_copy().wait_recv()
-        moe = cb_e[0, 0] + last[1].astype(jnp.float32)
-        outs[E] = (tokens[:, E * F :].astype(jnp.float32) + moe).astype(jnp.bfloat16)
-        pipe_copy(E).start()
-
+                cb_e[i, 0, 0] = total
+        late_copy(i).start()
+
+    def finish_e(i):
+        late_copy(i).wait_recv()
+        moe = cb_e[i, 0, 0] + last[i, 1].astype(jnp.float32)
+        part = pl.ds(pl.multiple_of((E + i) * F, F), F)
+        outs[E + i] = (tokens[:, part].astype(jnp.float32) + moe).astype(jnp.bfloat16)
+        pipe_copy(E + i).start()
+
+    def each_e(body):
+        def one(i, carry):
+            body(i)
+            return carry
+
+        lax.fori_loop(0, NE, one, 0)
+
+    sent(0, 0)
     for t in (2, 3, 1, 0):
+        for g in (0, 1):
+            if t:
+                x_copy(E - 1, t, g).wait_recv()
+            else:
+                x_own(E - 1, g).wait()
         act(t)
         produce_for(0, t)
-        for g in (1, 0):
-            if t:
-                y_copy(0, t, g).start()
-            else:
-                y_own(0, g).start()
-    produce_e()
-    unselect_e()
+        if t:
+            y_copy(0, t, 1).start()
+        else:
+            y_own(0, 1).start()
+    lax.fori_loop(1, E, sent, 0)
+    for i in range(NE):
+        for way in (0, 1):
+            for s in range(1, 5):
+                ze_copy(i, way, s).wait_send()
+        early_copy(i).wait_send()
+        xe_copy(i).wait_send()
+
+    produce(1)
+    each_e(produce_e)
+    each_e(unselect_e)
     LEAD = 3
-    for q in range(1, LEAD):
-        produce(q)
-
-    def span(tau, s, body):
+
+    def span(tau, d, body):
         def one(q, carry):
             body(q)
             return carry
 
-        high = jnp.where(tau == E - 2 + s, E, jnp.minimum(tau - s + 1, E - 1))
-        lax.fori_loop(jnp.maximum(tau - s, 0), high, one, 0)
+        high = jnp.where(tau == E - 2 + d, E, jnp.minimum(tau - d + 1, E - 1))
+        lax.fori_loop(jnp.maximum(tau - d, 0), high, one, 0)
 
     def combine_tick(tau, carry):
-        span(tau, 4, finish)
-        span(tau, 3, pass_on(3))
-        span(tau, 2, pass_on(2))
+        span(tau, 3, finish)
+        span(tau, 2, pass_on(3))
 
         @pl.when((tau >= 1) & (tau < E))
         def _():
-            pass_on(1)(tau - 1)
-
+            pass_on(2)(tau - 1)
+
+        valid(tau, pass_on(1))
         for s in (1, 2, 3):
 
             @pl.when(tau == s - 1)
             def _():
-                pass_on_e(s)
+                each_e(lambda i: pass_on_e(i, s))
 
         @pl.when(tau == 3)
         def _():
-            cross_e()
+            each_e(cross_e)
 
         @pl.when(tau == 5)
         def _():
-            finish_e()
-
-        valid(tau, unselect(1))
+            each_e(finish_e)
+
+        valid(tau + 1, unselect(1))
 
         @pl.when(tau + LEAD < E)
         def _():
             produce(tau + LEAD)
 
+        @pl.when(tau + LEAD == E)
+        def _():
+            give(E - 1, 0)
+
         valid(tau, unselect(0))
 
         @pl.when(tau == E - 1)
         def _():
-            pass_on(1)(tau)
+            pass_on(2)(tau)
 
         return carry
 
-    lax.fori_loop(0, E + 3, combine_tick, 0)
+    lax.fori_loop(-1, E + 2, combine_tick, 0)
 
     def drain(q, carry):
         for way in (0, 1):
-            for s in range(1, 5):
-                z_copy(q, way, s).wait_send()
             for s in range(4):
                 rs_copy(q, way, s).wait_send()
         for g in (0, 1):
@@ -580,19 +608,21 @@
         pipe_copy(q).wait()
         return carry
 
-    for d, col in pt_all:
-        for kind in (0, 1):
-            pt_copy(kind, d, col).wait_send()
-    for way in (0, 1):
-        for s in range(1, 5):
-            ze_copy(way, s).wait_send()
-        for s in range(4):
-            rse_copy(way, s).wait_send()
-    early_copy().wait_send()
-    late_copy().wait_send()
-    ye_copy().wait_send()
+    for kind in (0, 1):
+        for d in pt_all:
+            pt_copy(kind, d).wait_send()
+        pt_share(kind).wait_send()
+
+    def drain_e(i):
+        for way in (0, 1):
+            for s in range(4):
+                rse_copy(i, way, s).wait_send()
+        late_copy(i).wait_send()
+        ye_copy(i).wait_send()
+        pipe_copy(E + i).wait()
+
+    each_e(drain_e)
     lax.fori_loop(0, E, drain, 0)
-    pipe_copy(E).wait()
 
 
 def local(tokens, routes, norm_gain, router_weight, w_gate, w_up, w_down):
@@ -611,8 +641,8 @@
         out_specs=anywhere,
         scratch_shapes=[
             pltpu.VMEM((tok, width), bf),
-            pltpu.VMEM((nq - 1, NZ, tok, F), bf),
-            pltpu.VMEM((2, NZ, tok, F), bf),
+            pltpu.VMEM((nq - NE, NZ, tok, F), bf),
+            pltpu.VMEM((NE, 2, NZ, tok, F), bf),
             pltpu.VMEM((NZ, 16, tok), bf),
             pltpu.VMEM((NZ, 16, tok), bf),
             pltpu.VMEM((2, NZ, 16, tok), bf),
@@ -623,18 +653,16 @@
             pltpu.VMEM((2, 2, GROUP * tok, 2 * ROWS), bf),
             pltpu.VMEM((nq, 4, 2, ROWS, F), bf),
             pltpu.VMEM((nq, 2, 2, 2, ROWS, F), bf),
-            pltpu.VMEM((nq - 1, 2, 4, ROWS, F), bf),
-            pltpu.VMEM((2, 2, 2, ROWS, F), bf),
+            pltpu.VMEM((nq - NE, 2, 4, ROWS, F), bf),
+            pltpu.VMEM((NE, 2, 2, 2, ROWS, F), bf),
             pltpu.VMEM((8 * ROWS, ff), f32),
             pltpu.VMEM((8 * ROWS, ff), f32),
             pltpu.VMEM((8 * ROWS, ff), bf),
             pltpu.VMEM((KEPT, 7, tok, F), f32),
-            pltpu.VMEM((2, 7, tok, F), f32),
-            pltpu.VMEM((nq - 1, 2, 4, tok, F), bf),
-            pltpu.VMEM((nq - 1, 2, 4, tok, F), bf),
-            pltpu.VMEM((2, 4, 2, tok, F), bf),
-            pltpu.VMEM((2, 4, 2, tok, F), bf),
-            pltpu.VMEM((2, tok, F), bf),
+            pltpu.VMEM((NE, 2, 7, tok, F), f32),
+            pltpu.VMEM((nq - NE, 2, 4, tok, F), bf),
+            pltpu.VMEM((NE, 2, 4, 2, tok, F), bf),
+            pltpu.VMEM((NE, 2, tok, F), bf),
             pltpu.VMEM((nq, tok, F), bf),
             pltpu.VMEM((width, ff), bf),
             pltpu.VMEM((width, ff), bf),
@@ -649,8 +677,8 @@
             dma((nq, 4, 2)),
             dma((nq, 2, 4)),
             dma((nq, 2, 4)),
-            dma((2,)),
-            dma((2,)),
+            dma((NE, 2)),
+            dma((NE, 2)),
             dma((nq,)),
             dma((nq,)),
             dma((4,)),

time: 147 us -> 144 us (0.980)
  Pallas kernels: 144 us -> 142 us
    pallas_call x1, Pallas kernels: 144 us -> 142 us  [local(): pl.pallas_call(functools.partial(kernel, nq), out_shape=jax.ShapeDtypeStr...]
where the time goes in v4:
time: 144 us; the launch traced here: 143 us
  Pallas kernels  142 us (99%)
  local copies, waits for them, and re-layouts  1.88 us (1%)
    pallas_call x1, Pallas kernels, local(): pl.pallas_call(functools.partial(kernel, nq), out_shape=jax.ShapeDtypeStr...  142 us

profile of v4, /device:TPU:2, one launch (start us, length us, event | category | flops | bytes accessed | tf_op | source)
XLA Modules:
  0.0 143.5 jit_solution(14483826021067238611)
XLA Ops:
  0.0 141.6 %relay_moe.1 = bf16[1,128,2048]{2,1,0:T(8,128)(2,1)} custom-call(bf16[1,128,2048]{2,1,0:T(8,128)(2,1)} %tok_hbm.1, s32[6,1,128]{2,1,0:T(1,128)} %bitcast.3, f32[1,2048]{1,0:T(1,128)} %gain.1, bf16[1,32,2048]{2,1,0:T(8,128)(2,1)} %bitcast.2, bf16[1,1,2048,768]{3,2,1,0:T(8,128)(2,1)} %wg_hbm.1, bf16[1,1,2048,768]{3,2,1,0:T(8,128)(2,1)} %wu_hbm.1, ...), custom_call_target="tpu_custom_call" | custom-call | tf_op jit(solution)/shard_map/relay_moe/pallas_call | solution.py:637
  141.6 1.9 %copy.9 = bf16[1,128,2048]{2,1,0:T(8,128)(2,1)} copy(bf16[1,128,2048]{2,1,0:T(8,128)(2,1)} %relay_moe.1) | data formatting | bytes 1048576

commit v5 on v4

--- a/solution.py
+++ b/solution.py
@@ -305,6 +305,14 @@
                 x_copy(q, t, g).wait_recv()
             x_own(q, g).wait()
 
+    def sent(q):
+        for way in (0, 1):
+            for s in range(1, 5):
+                z_copy(q, way, s).wait_send()
+        for g in (0, 1):
+            for t in (1, 2, 3):
+                x_copy(q, t, g).wait_send()
+
     LAG = 3
 
     def gather_tick(tau, carry):
@@ -333,6 +341,7 @@
 
         def take(q):
             receive(q)
+            sent(q)
             multiply(q)
 
         @pl.when((tau - 4 - LAG >= 0) & (tau - 4 - LAG < E - 1))
@@ -367,15 +376,6 @@
     build_wmap(1)
     lax.fori_loop(9, max(nq + 5, E + 3 + LAG), gather_tick, 0)
 
-    def sent(q, carry):
-        for way in (0, 1):
-            for s in range(1, 5):
-                z_copy(q, way, s).wait_send()
-        for g in (0, 1):
-            for t in (1, 2, 3):
-                x_copy(q, t, g).wait_send()
-        return carry
-
     sides = [(a, c), (a, 1 - c), (1 - a, c), (1 - a, 1 - c)]
 
     def act(t):
@@ -521,7 +521,6 @@
 
         lax.fori_loop(0, NE, one, 0)
 
-    sent(0, 0)
     for t in (2, 3, 1, 0):
         for g in (0, 1):
             if t:
@@ -534,7 +533,7 @@
             y_copy(0, t, 1).start()
         else:
             y_own(0, 1).start()
-    lax.fori_loop(1, E, sent, 0)
+    sent(E - 1)
     for i in range(NE):
         for way in (0, 1):
             for s in range(1, 5):
@@ -545,7 +544,8 @@
     produce(1)
     each_e(produce_e)
     each_e(unselect_e)
-    LEAD = 3
+    produce(2)
+    LEAD = 4
 
     def span(tau, d, body):
         def one(q, carry):
@@ -555,63 +555,14 @@
         high = jnp.where(tau == E - 2 + d, E, jnp.minimum(tau - d + 1, E - 1))
         lax.fori_loop(jnp.maximum(tau - d, 0), high, one, 0)
 
-    def combine_tick(tau, carry):
-        span(tau, 3, finish)
-        span(tau, 2, pass_on(3))
-
-        @pl.when((tau >= 1) & (tau < E))
-        def _():
-            pass_on(2)(tau - 1)
-
-        valid(tau, pass_on(1))
-        for s in (1, 2, 3):
-
-            @pl.when(tau == s - 1)
-            def _():
-                each_e(lambda i: pass_on_e(i, s))
-
-        @pl.when(tau == 3)
-        def _():
-            each_e(cross_e)
-
-        @pl.when(tau == 5)
-        def _():
-            each_e(finish_e)
-
-        valid(tau + 1, unselect(1))
-
-        @pl.when(tau + LEAD < E)
-        def _():
-            produce(tau + LEAD)
-
-        @pl.when(tau + LEAD == E)
-        def _():
-            give(E - 1, 0)
-
-        valid(tau, unselect(0))
-
-        @pl.when(tau == E - 1)
-        def _():
-            pass_on(2)(tau)
-
-        return carry
-
-    lax.fori_loop(-1, E + 2, combine_tick, 0)
-
-    def drain(q, carry):
+    def drain(q):
         for way in (0, 1):
             for s in range(4):
                 rs_copy(q, way, s).wait_send()
         for g in (0, 1):
             for t in (1, 2, 3):
                 y_copy(q, t, g).wait_send()
-        pipe_copy(q).wait()
-        return carry
-
-    for kind in (0, 1):
-        for d in pt_all:
-            pt_copy(kind, d).wait_send()
-        pt_share(kind).wait_send()
+        pipe_copy(q).wait_send()
 
     def drain_e(i):
         for way in (0, 1):
@@ -619,10 +570,71 @@
                 rse_copy(i, way, s).wait_send()
         late_copy(i).wait_send()
         ye_copy(i).wait_send()
-        pipe_copy(E + i).wait()
-
-    each_e(drain_e)
-    lax.fori_loop(0, E, drain, 0)
+        pipe_copy(E + i).wait_send()
+
+    def combine_tick(tau, carry):
+        span(tau, 3, finish)
+        span(tau, 2, pass_on(3))
+
+        @pl.when((tau >= 1) & (tau < E))
+        def _():
+            pass_on(2)(tau - 1)
+
+        valid(tau, pass_on(1))
+        for s in (1, 2, 3):
+
+            @pl.when(tau == s - 1)
+            def _():
+                each_e(lambda i: pass_on_e(i, s))
+
+        @pl.when(tau == 3)
+        def _():
+            each_e(cross_e)
+
+        @pl.when(tau == 5)
+        def _():
+            each_e(finish_e)
+
+        valid(tau + 1, unselect(1))
+
+        @pl.when(tau + LEAD < E)
+        def _():
+            produce(tau + LEAD)
+
+        @pl.when(tau + LEAD == E)
+        def _():
+            give(E - 1, 0)
+
+        valid(tau, unselect(0))
+
+        @pl.when(tau == E - 1)
+        def _():
+            pass_on(2)(tau)
+
+        @pl.when((tau >= 4) & (tau - 4 < E - 2))
+        def _():
+            drain(tau - 4)
+
+        @pl.when(tau == 6)
+        def _():
+            each_e(drain_e)
+            for kind in (0, 1):
+                for d in pt_all:
+                    pt_copy(kind, d).wait_send()
+                pt_share(kind).wait_send()
+
+        return carry
+
+    lax.fori_loop(-1, E + 2, combine_tick, 0)
+
+    for q in (E - 2, E - 1):
+        drain(q)
+
+    def arrive(q, carry):
+        pipe_copy(q).wait_recv()
+        return carry
+
+    lax.fori_loop(0, nq, arrive, 0)
 
 
 def local(tokens, routes, norm_gain, router_weight, w_gate, w_up, w_down):

time: 144 us -> 145 us (level)
  no operation moved by 1% of the time
where the time goes in v5:
time: 145 us
  Pallas kernels  143 us (99%)
  local copies, waits for them, and re-layouts  1.88 us (1%)
    pallas_call x1, Pallas kernels, local(): pl.pallas_call(functools.partial(kernel, nq), out_shape=jax.ShapeDtypeStr...  143 us

profile of v5, /device:TPU:2, one launch (start us, length us, event | category | flops | bytes accessed | tf_op | source)
XLA Modules:
  0.0 144.9 jit_solution(14034683327342489103)
XLA Ops:
  0.0 143.0 %relay_moe.1 = bf16[1,128,2048]{2,1,0:T(8,128)(2,1)} custom-call(bf16[1,128,2048]{2,1,0:T(8,128)(2,1)} %tok_hbm.1, s32[6,1,128]{2,1,0:T(1,128)} %bitcast.3, f32[1,2048]{1,0:T(1,128)} %gain.1, bf16[1,32,2048]{2,1,0:T(8,128)(2,1)} %bitcast.2, bf16[1,1,2048,768]{3,2,1,0:T(8,128)(2,1)} %wg_hbm.1, bf16[1,1,2048,768]{3,2,1,0:T(8,128)(2,1)} %wu_hbm.1, ...), custom_call_target="tpu_custom_call" | custom-call | tf_op jit(solution)/shard_map/relay_moe/pallas_call | solution.py:649
  143.1 1.9 %copy.9 = bf16[1,128,2048]{2,1,0:T(8,128)(2,1)} copy(bf16[1,128,2048]{2,1,0:T(8,128)(2,1)} %relay_moe.1) | data formatting | bytes 1048576
